TPU v7x, 128 devices: a whole 4x4x4 slice. The times are simulated.
128 devices in a mesh: frames: 16 (over x, y_lo, core), pairs: 8 (over y_hi, z).
Axes of the slice: x: 4, y: 4 (y_hi: 2, y_lo: 2; y = y_hi * 2 + y_lo), z: 4, core: 2. Of those that a mesh axis runs over, the one named last changes fastest.
Arguments:
- coords: float32 [8192, 3, 384], P('frames'), may hold values from -3 to 3
- pair_first: int32 [512], P('pairs'), may hold values from 0 to 383
- pair_second: int32 [65536], P('pairs'), may hold values from 0 to 383
- enc_weight: bfloat16 [64, 65536], P(None, 'pairs'), may hold values from -0.0234375 to 0.0234375
- enc_bias: float32 [64], replicated, may hold values from -4 to 4
- dec_weight: bfloat16 [64, 65536], P(None, 'pairs'), may hold values from -0.75 to 0.75
- dec_bias: float32 [65536], P('pairs'), may hold values from -3 to 3
- lag_frames: int32 [1], replicated, may hold values from 256 to 512
Outputs:
- grad_enc: float32 [64, 65536], P(None, 'pairs')
- grad_dec: float32 [64, 65536], P(None, 'pairs')
Inputs may be any that keep to these rules, and one draw needn't show every extreme that they name: Residue numbers; pair p joins residue pair_first[p // 128] with residue pair_second[p].
All inputs are finite; a program needn't handle non-finite values.
Results may differ from a plain program's by a relative error of at most 0.0003.
Values may be sent and summed in bfloat16 or wider, within the bound.
No kernel may reach another device: no remote copies, remote signals or barrier semaphores. Data moves between devices by JAX's collectives and lax.ppermute only.
A program may use at most 192 MiB of HBM per device.

v0:
```python
import functools
import math

import jax
import jax.numpy as jnp
from jax import lax
from jax.experimental import pallas as pl
from jax.experimental.pallas import tpu as pltpu
from jax.sharding import PartitionSpec as P


cutoff_dist = 2.3
softness = 0.4
LANES = 128
BF = jnp.bfloat16
F32 = jnp.float32


def params(mib):
    return pltpu.CompilerParams(dimension_semantics=("arbitrary",), vmem_limit_bytes=mib << 20)


scaling = 1.0 / (softness * math.log(2.0))
CHUNK = 64


def contact_kernel(first_ref, second_ref, coords_ref, enc_ref, contact_ref, sum_ref, table, total):
    frames, residues = coords_ref.shape[1:]
    width = contact_ref.shape[1]
    block = pl.program_id(0)

    @pl.when(block == 0)
    def _():
        for c in range(3):
            value = coords_ref[c] * scaling
            high = value.astype(BF)
            low = (value - high.astype(F32)).astype(BF)
            for i in range(frames // CHUNK):
                rows = slice((3 * i + c) * CHUNK, (3 * i + c + 1) * CHUNK)
                table[rows, :residues] = high[i * CHUNK:(i + 1) * CHUNK]
                table[rows, residues:] = low[i * CHUNK:(i + 1) * CHUNK]
        total[...] = jnp.zeros_like(total)

    picks = []
    for g in range(width // LANES):
        rows = lax.broadcasted_iota(jnp.int32, (residues, LANES), 0)
        second = second_ref[:, g * LANES:(g + 1) * LANES]
        first = first_ref[block * (width // LANES) + g]
        far = jnp.where(rows == second, 1.0, 0.0)
        near = jnp.where(rows == first, 1.0, 0.0)
        picks.append((far - near).astype(BF))
    pick = jnp.concatenate(picks, axis=1)
    pick = jnp.concatenate([pick, pick], axis=0)
    offset = jnp.dot(table[...], pick, preferred_element_type=F32)
    parts = []
    for i in range(frames // CHUNK):
        x, y, z = (offset[(3 * i + c) * CHUNK:(3 * i + c + 1) * CHUNK] for c in range(3))
        square = x * x + y * y + z * z
        distance = square * lax.rsqrt(jnp.maximum(square, 1e-30))
        below = 1.0 + jnp.exp2(distance - cutoff_dist * scaling)
        value = pl.reciprocal(below, approx=True)
        parts.append((value * (2.0 - below * value)).astype(BF))
    contact = jnp.concatenate(parts, axis=0)
    contact_ref[...] = contact
    total[...] += lax.dot_general(
        enc_ref[...], contact, (((1,), (1,)), ((), ())), preferred_element_type=F32
    )

    @pl.when(block == pl.num_programs(0) - 1)
    def _():
        sum_ref[...] = total[...]


def contacts_and_sum(coords, first, second, enc, width):
    _, frames, residues = coords.shape
    latents, pairs = enc.shape
    return pl.pallas_call(
        contact_kernel,
        grid_spec=pltpu.PrefetchScalarGridSpec(
            num_scalar_prefetch=1,
            grid=(pairs // width,),
            in_specs=[
                pl.BlockSpec((1, width), lambda j, s: (0, j)),
                pl.BlockSpec((3, frames, residues), lambda j, s: (0, 0, 0)),
                pl.BlockSpec((latents, width), lambda j, s: (0, j)),
            ],
            out_specs=[
                pl.BlockSpec((frames, width), lambda j, s: (0, j)),
                pl.BlockSpec((latents, frames), lambda j, s: (0, 0)),
            ],
            scratch_shapes=[
                pltpu.VMEM((3 * frames, 2 * residues), BF),
                pltpu.VMEM((latents, frames), F32),
            ],
        ),
        out_shape=[
            jax.ShapeDtypeStruct((frames, pairs), BF),
            jax.ShapeDtypeStruct((latents, frames), F32),
        ],
        compiler_params=params(56),
        name="contacts",
    )(first, second.reshape(1, pairs), coords, enc)


GROUPS = 8


def write_groups(out_ref, grad, chip):
    for k in range(GROUPS):
        row = pl.multiple_of(jnp.bitwise_xor(chip, k) * 8, 8)
        out_ref[k] = grad[pl.ds(row, 8), :]


def decode_kernel(
    info_ref, scale_ref, latent_ref, before_ref, dec_ref, bias_ref, contact_ref,
    keep_ref, give_ref, back_ref, rolled, rolled_t, scale_col, grad, back,
):
    latents, frames = latent_ref.shape
    lag, is_first, chip = info_ref[0], info_ref[1], info_ref[3]
    block, blocks = pl.program_id(0), pl.num_programs(0)

    @pl.when(block == 0)
    def _():
        own = pltpu.roll(latent_ref[...].astype(F32), lag, 1)
        before = pltpu.roll(before_ref[...].astype(F32), lag, 1)
        frame = lax.broadcasted_iota(jnp.int32, (latents, frames), 1)
        value = jnp.where(frame >= lag, own, before)
        rolled[...] = value.astype(BF)
        rolled_t[:, :latents] = value.T.astype(BF)
        column = lax.broadcasted_iota(jnp.int32, (frames, 16), 1)
        rolled_t[:, latents:] = jnp.where(column < 3, 1.0, 0.0).astype(BF)
        row = lax.broadcasted_iota(jnp.int32, (frames, LANES), 0)
        scale_col[...] = jnp.where((row < lag) & (is_first == 1), 0.0, scale_ref[0])
        back[...] = jnp.zeros_like(back)

    dec = dec_ref[...]
    width = dec.shape[1]
    bias = bias_ref[...]
    high = bias.astype(BF).astype(F32)
    middle = (bias - high).astype(BF).astype(F32)
    low = bias - high - middle
    row = lax.broadcasted_iota(jnp.int32, (16, width), 0)
    rows = jnp.where(row == 0, high, jnp.where(row == 1, middle, jnp.where(row == 2, low, 0.0)))
    weights = jnp.concatenate([dec, rows.astype(BF)], axis=0)
    decoded = jnp.dot(rolled_t[...], weights, preferred_element_type=F32)
    scale = jnp.concatenate([scale_col[...]] * (width // LANES), axis=1)
    err = ((decoded - contact_ref[...].astype(F32)) * scale).astype(BF)
    grad[...] = jnp.dot(rolled[...], err, preferred_element_type=F32)

    @pl.when(block < blocks // 2)
    def _():
        write_groups(give_ref, grad, chip)

    @pl.when(block >= blocks // 2)
    def _():
        write_groups(keep_ref, grad, chip)

    back[...] += lax.dot_general(dec, err, (((1,), (1,)), ((), ())), preferred_element_type=F32)

    @pl.when(block == blocks - 1)
    def _():
        back_ref[...] = pltpu.roll(back[...], lax.rem(frames - lag, frames), 1)


def decode(info, scale, latent, before, dec, bias, contact, blocks):
    latents, frames = latent.shape
    pairs = dec.shape[1]
    width = pairs // blocks
    per = blocks // 2
    col = lambda j, s, f: (0, jnp.where(j < per, 1 - s[2], s[2]) * per + lax.rem(j, per))
    whole = lambda j, s, f: (0, 0)
    return pl.pallas_call(
        decode_kernel,
        grid_spec=pltpu.PrefetchScalarGridSpec(
            num_scalar_prefetch=2,
            grid=(blocks,),
            in_specs=[
                pl.BlockSpec((latents, frames), whole),
                pl.BlockSpec((latents, frames), whole),
                pl.BlockSpec((latents, width), col),
                pl.BlockSpec((1, width), col),
                pl.BlockSpec((frames, width), col),
            ],
            out_specs=[
                pl.BlockSpec((GROUPS, 8, width), lambda j, s, f: (0, 0, jnp.maximum(j - per, 0))),
                pl.BlockSpec((GROUPS, 8, width), lambda j, s, f: (0, 0, jnp.minimum(j, per - 1))),
                pl.BlockSpec((latents, frames), whole),
            ],
            scratch_shapes=[
                pltpu.VMEM((latents, frames), BF),
                pltpu.VMEM((frames, latents + 16), BF),
                pltpu.VMEM((frames, LANES), F32),
                pltpu.VMEM((latents, width), F32),
                pltpu.VMEM((latents, frames), F32),
            ],
        ),
        out_shape=[
            jax.ShapeDtypeStruct((GROUPS, 8, pairs // 2), F32),
            jax.ShapeDtypeStruct((GROUPS, 8, pairs // 2), F32),
            jax.ShapeDtypeStruct((latents, frames), F32),
        ],
        compiler_params=params(56),
        name="decode",
    )(info, scale, latent, before, dec, bias.reshape(1, pairs), contact)


def encode_kernel(info_ref, hidden_ref, contact_ref, out_ref, grad):
    grad[...] = jnp.dot(hidden_ref[...], contact_ref[...], preferred_element_type=F32)
    write_groups(out_ref, grad, info_ref[3])


def encode(info, hidden, contact, blocks, other):
    latents, frames = hidden.shape
    half = contact.shape[1] // 2
    width = half // blocks
    return pl.pallas_call(
        encode_kernel,
        grid_spec=pltpu.PrefetchScalarGridSpec(
            num_scalar_prefetch=1,
            grid=(blocks,),
            in_specs=[
                pl.BlockSpec((latents, frames), lambda j, s: (0, 0)),
                pl.BlockSpec(
                    (frames, width),
                    lambda j, s: (0, (1 - s[2] if other else s[2]) * blocks + j),
                ),
            ],
            out_specs=pl.BlockSpec((GROUPS, 8, width), lambda j, s: (0, 0, j)),
            scratch_shapes=[pltpu.VMEM((latents, width), F32)],
        ),
        out_shape=jax.ShapeDtypeStruct((GROUPS, 8, half), F32),
        compiler_params=params(20),
        name="encode_other_half" if other else "encode_own_half",
    )(info, hidden, contact)


def assemble_kernel(layout, info_ref, *refs):
    pieces, out_refs, sems = refs[:-3][-len(layout):], refs[-3:-1], refs[-1]
    core, chip = info_ref[2], info_ref[3]
    half = out_refs[0].shape[1] // 2
    copies = []
    for ref, (mine, first_col, codes) in zip(pieces, layout):
        side = core if mine else 1 - core
        for m, code in enumerate(codes):
            row = pl.multiple_of(jnp.bitwise_xor(chip, code) * 8, 8)
            col = pl.multiple_of(side * half + first_col, LANES)
            for n, out_ref in enumerate(out_refs):
                copies.append(
                    pltpu.make_async_copy(
                        ref.at[m, n],
                        out_ref.at[pl.ds(row, 8), pl.ds(col, ref.shape[3])],
                        sems.at[len(copies)],
                    )
                )
    for copy in copies:
        copy.start()
    for copy in copies:
        copy.wait()


def assemble(info, pieces, layout, shape, begun=()):
    count = 2 * sum(len(codes) for _, _, codes in layout)
    spec = pl.BlockSpec(memory_space=pl.ANY)
    return pl.pallas_call(
        functools.partial(assemble_kernel, layout),
        grid_spec=pltpu.PrefetchScalarGridSpec(
            num_scalar_prefetch=1,
            grid=(1,),
            in_specs=[spec] * (len(begun) + len(pieces)),
            out_specs=[spec] * 2,
            scratch_shapes=[pltpu.SemaphoreType.DMA((count,))],
        ),
        out_shape=[jax.ShapeDtypeStruct(shape, F32)] * 2,
        input_output_aliases={1 + n: n for n in range(len(begun))},
        compiler_params=params(2),
        name="assemble_rest" if begun else "assemble",
    )(info, *begun, *pieces)


GRAY = (0, 2, 3, 1)


def chip_code(place):
    x, y = place // 4, (place // 2) % 2
    return y * 4 + jnp.where((x == 1) | (x == 2), 2, 0) + jnp.where(x >= 2, 1, 0)


def flip(value, bit):
    route = []
    for i in range(16):
        x, y, core = i // 4, (i // 2) % 2, i % 2
        code = (y * 4 + GRAY[x]) ^ bit
        route.append((i, GRAY.index(code % 4) * 4 + (code // 4) * 2 + core))
    return lax.ppermute(value, "frames", route)


def swap_cores(value):
    return lax.ppermute(value, "frames", [(i, i ^ 1) for i in range(16)])


AXIS_OF = {4: 0, 2: 1, 1: 2}


def scatter(kept, got, parts):
    half = kept[0].shape[2]
    shape = (2, 2, 2, 8, half)
    held = []
    for start, stop, order in parts:
        axes = [AXIS_OF[b] for b in order] + [3, 4]
        arrays = [
            (k.reshape(shape)[..., start:stop] + g.reshape(shape)[..., start:stop]).transpose(axes)
            for k, g in zip(kept, got)
        ]
        held.append(jnp.stack(arrays, axis=3))
    for step in range(3):
        sent = []
        for v, (_, _, order) in zip(held, parts):
            sent.append(flip(v[1], order[step]))
        held = [v[0] + s for v, s in zip(held, sent)]
    return held


def gather(held, parts, half, info):
    for step in (2, 1, 0):
        sent = []
        for v, (_, _, order) in zip(held, parts):
            sent.append(flip(v, order[step]))
        if step > 0:
            held = [jnp.stack([v, s]) for v, s in zip(held, sent)]
    early, late = ([], []), ([], [])
    for v, s, (start, stop, order) in zip(held, sent, parts):
        for array, lead in ((v, 0), (s, order[0])):
            codes = tuple(lead + b1 * order[1] + b2 * order[2] for b1 in (0, 1) for b2 in (0, 1))
            array = array.reshape(4, 2, 8, stop - start)
            swapped = swap_cores(array)
            for mine, piece in ((True, array), (False, swapped)):
                pieces, layout = late if lead else early
                pieces.append(piece)
                layout.append((mine, start, codes))
    begun = assemble(info, early[0], tuple(early[1]), (64, 2 * half))
    return assemble(info, late[0], tuple(late[1]), (64, 2 * half), begun)


def small_call(body, outs, *arrays):
    return pl.pallas_call(
        body,
        out_shape=[jax.ShapeDtypeStruct(shape, kind) for shape, kind in outs],
        compiler_params=pltpu.CompilerParams(vmem_limit_bytes=4 << 20),
    )(*arrays)


def add_kernel(a_ref, b_ref, out_ref):
    out_ref[...] = a_ref[...] + b_ref[...]


def add_four_kernel(a_ref, b_ref, c_ref, d_ref, out_ref):
    out_ref[...] = (a_ref[...] + b_ref[...]) + (c_ref[...] + d_ref[...])


def latent_kernel(a_ref, b_ref, c_ref, d_ref, bias_ref, latent_ref, rounded_ref):
    total = (a_ref[...] + b_ref[...]) + (c_ref[...] + d_ref[...])
    latent = jnp.tanh(total + bias_ref[...])
    latent_ref[...] = latent
    rounded_ref[...] = latent.astype(BF)


def hidden_kernel(back_ref, after_ref, latent_ref, last_ref, hidden_ref):
    frame = lax.broadcasted_iota(jnp.int32, back_ref.shape, 1)
    backward = jnp.where(frame < last_ref[...], back_ref[...], after_ref[...])
    latent = latent_ref[...]
    hidden_ref[...] = (backward * (1.0 - latent * latent)).astype(BF)


def terms_over_pairs(value):
    got = lax.ppermute(value, "pairs", [(i, i ^ 4) for i in range(8)])
    (value,) = small_call(add_kernel, [(value.shape, F32)], value, got)
    terms = [value]
    for k in (1, 3, 2):
        route = [(i, (i // 4) * 4 + (i + k) % 4) for i in range(8)]
        terms.append(lax.ppermute(value, "pairs", route))
    return terms


def local(coords, pair_first, pair_second, enc_weight, enc_bias, dec_weight, dec_bias, lag_frames):
    frame_rows = coords.shape[0]
    devices = lax.axis_size("frames")
    total_frames = frame_rows * devices
    lag = lag_frames[0]
    place = lax.axis_index("frames")
    info = jnp.stack([lag, (place == 0).astype(jnp.int32), place % 2, chip_code(place)])
    info = info.astype(jnp.int32)
    scale = (1.0 / jnp.sqrt(jnp.float32(total_frames) - lag.astype(F32))).reshape(1)
    bias = enc_bias[:, None]
    last = (frame_rows - lag).reshape(1, 1)
    pair_first, info, scale, bias, last = lax.optimization_barrier(
        (pair_first, info, scale, bias, last)
    )

    contact, partial_sum = contacts_and_sum(
        jnp.transpose(coords, (1, 0, 2)), pair_first, pair_second, enc_weight, 2048
    )
    whole = partial_sum.shape
    latent, latent_bf = small_call(
        latent_kernel, [(whole, F32), (whole, BF)],
        *terms_over_pairs(partial_sum), bias,
    )
    before = lax.ppermute(latent_bf, "frames", [(i, i + 1) for i in range(devices - 1)])
    dec_keep, give, back_terms = decode(
        info, scale, latent_bf, before, dec_weight, dec_bias, contact, 4
    )
    dec_got = swap_cores(give)
    (rolled_back,) = small_call(add_four_kernel, [(whole, F32)], *terms_over_pairs(back_terms))
    after = lax.ppermute(rolled_back, "frames", [(i + 1, i) for i in range(devices - 1)])
    (hidden_bf,) = small_call(hidden_kernel, [(whole, BF)], rolled_back, after, latent, last)
    give = encode(info, hidden_bf, contact, 2, True)
    got = swap_cores(give)
    keep = encode(info, hidden_bf, contact, 2, False)
    held = scatter([keep, dec_keep], [got, dec_got], PARTS)
    return tuple(gather(held, PARTS, keep.shape[2], info))


PARTS = ((0, 1408, (4, 2, 1)), (1408, 2816, (2, 1, 4)), (2816, 4096, (1, 4, 2)))


def solution(mesh):
    placed = (
        P("frames", None, None),
        P("pairs"),
        P("pairs"),
        P(None, "pairs"),
        P(),
        P(None, "pairs"),
        P("pairs"),
        P(),
    )
    return jax.shard_map(
        local,
        mesh=mesh,
        in_specs=placed,
        out_specs=(P(None, "pairs"), P(None, "pairs")),
        check_vma=False,
    )
```

profile of v0, /device:TPU:0, one launch (start us, length us, event | category | flops | bytes accessed | tf_op | source)
XLA Modules:
  0.0 157.2 jit_solution(1965426990130962938)
XLA Ops:
  1.4 0.7 pad_add_fusion.info_ref
  2.0 29.7 %contacts.1 = (bf16[512,8192]{1,0:T(8,128)(2,1)}, f32[64,512]{1,0:T(8,128)}) custom-call(s32[64]{0:T(128)} %first_ref, s32[1,8192]{1,0:T(1,128)} %bitcast.137, f32[3,512,384]{2,1,0:T(8,128)} %bitcast.121, bf16[64,8192]{1,0:T(8,128)(2,1)} %enc_ref.1), custom_call_target="tpu_custom_call" | custom-call | tf_op jit(solution)/shard_map/contacts/pallas_call | solution.py:77
  31.7 3.3 %collective-permute-start = (f32[64,512]{1,0:T(8,128)}, f32[64,512]{1,0:T(8,128)S(1)}, u32[]{:S(2)}, u32[]{:S(2)}) collective-permute-start(f32[64,512]{1,0:T(8,128)} %get-tuple-element.19.a_ref), channel_id=1, source_target_pairs={{0,4},{1,5},{2,6},{3,7},{4,0},{5,1},{6,2},{7,3},{8,12},{9,13},{10,... | collective-permute-start | bytes 393224 | tf_op jit(solution)/shard_map/ppermute | solution.py:375
  35.0 3.7 %collective-permute-done.b_ref = f32[64,512]{1,0:T(8,128)S(1)} collective-permute-done((f32[64,512]{1,0:T(8,128)}, f32[64,512]{1,0:T(8,128)S(1)}, u32[]{:S(2)}, u32[]{:S(2)}) %collective-permute-start) | collective-permute-done | bytes 131104 | tf_op jit(solution)/shard_map/ppermute | solution.py:375
  38.7 0.9 copy-done.2
  39.7 4.0 %collective-permute-start.3 = (f32[64,512]{1,0:T(8,128)S(1)}, f32[64,512]{1,0:T(8,128)S(1)}, u32[]{:S(2)}, u32[]{:S(2)}) collective-permute-start(f32[64,512]{1,0:T(8,128)S(1)} %shard_map.95.a_ref), channel_id=1, source_target_pairs={{0,2},{1,3},{2,0},{3,1},{4,6},{5,7},{6,4},{7,5},{8,10},{9,11},{10,... | collective-permute-start | bytes 393224 | tf_op jit(solution)/shard_map/ppermute | solution.py:380
  43.7 0.7 collective-permute-start.2
  44.4 1.3 collective-permute-start.1
  45.8 1.4 collective-permute-done.3.d_ref
  47.2 2.7 %collective-permute-done.2.c_ref = f32[64,512]{1,0:T(8,128)S(1)} collective-permute-done((f32[64,512]{1,0:T(8,128)S(1)}, f32[64,512]{1,0:T(8,128)S(1)}, u32[]{:S(2)}, u32[]{:S(2)}) %collective-permute-start.2) | collective-permute-done | bytes 131104 | tf_op jit(solution)/shard_map/ppermute | solution.py:380
  49.9 0.7 collective-permute-done.1.b_ref
  50.7 1.3 collective-permute-start.4
  52.0 0.9 collective-permute-done.4.before_ref
  52.9 0.6 copy-done.6
  53.5 11.7 %decode.1 = (f32[8,8,4096]{2,1,0:T(8,128)}, f32[8,8,4096]{2,1,0:T(8,128)}, f32[64,512]{1,0:T(8,128)}) custom-call(s32[4]{0:T(128)} %pad_add_fusion.info_ref, f32[1]{0:T(128)S(6)} %sqrt.3.scale_ref, bf16[64,512]{1,0:T(8,128)(2,1)} %copy-done.3, bf16[64,512]{1,0:T(8,128)(2,1)} %copy-done.6, bf16[64,8192]{1,0:T(8,128)(2,1)} %dec_ref.1, f32[1,8192]{1,0:T(1,128)} %bitcast.138, ...), custom_call_target="tpu_custom_call" | custom-call | tf_op jit(solution)/shard_map/decode/pallas_call | solution.py:172
  65.1 2.8 %collective-permute-start.11 = (f32[8,8,4096]{2,1,0:T(8,128)}, f32[8,8,4096]{2,1,0:T(8,128)S(1)}, u32[]{:S(2)}, u32[]{:S(2)}) collective-permute-start(f32[8,8,4096]{2,1,0:T(8,128)} %get-tuple-element.27), channel_id=1, source_target_pairs={{0,8},{8,0},{16,24},{24,16},{32,40},{40,32},{48,56},{56,48},{64,72... | collective-permute-start | bytes 3145736 | tf_op jit(solution)/shard_map/ppermute | solution.py:298
  68.0 2.9 %collective-permute-start.5 = (f32[64,512]{1,0:T(8,128)}, f32[64,512]{1,0:T(8,128)S(1)}, u32[]{:S(2)}, u32[]{:S(2)}) collective-permute-start(f32[64,512]{1,0:T(8,128)} %get-tuple-element.23.a_ref), channel_id=1, source_target_pairs={{0,4},{1,5},{2,6},{3,7},{4,0},{5,1},{6,2},{7,3},{8,12},{9,13},{10,... | collective-permute-start | bytes 393224 | tf_op jit(solution)/shard_map/ppermute | solution.py:375
  70.9 4.3 %collective-permute-done.5.b_ref = f32[64,512]{1,0:T(8,128)S(1)} collective-permute-done((f32[64,512]{1,0:T(8,128)}, f32[64,512]{1,0:T(8,128)S(1)}, u32[]{:S(2)}, u32[]{:S(2)}) %collective-permute-start.5) | collective-permute-done | bytes 131104 | tf_op jit(solution)/shard_map/ppermute | solution.py:375
  75.2 0.9 copy-done.1
  76.1 1.9 %collective-permute-start.8 = (f32[64,512]{1,0:T(8,128)S(1)}, f32[64,512]{1,0:T(8,128)S(1)}, u32[]{:S(2)}, u32[]{:S(2)}) collective-permute-start(f32[64,512]{1,0:T(8,128)S(1)} %shard_map.97.a_ref), channel_id=1, source_target_pairs={{0,2},{1,3},{2,0},{3,1},{4,6},{5,7},{6,4},{7,5},{8,10},{9,11},{10,... | collective-permute-start | bytes 393224 | tf_op jit(solution)/shard_map/ppermute | solution.py:380
  78.0 1.2 collective-permute-start.7
  79.2 0.8 collective-permute-start.6
  80.0 3.9 %collective-permute-done.8.d_ref = f32[64,512]{1,0:T(8,128)S(1)} collective-permute-done((f32[64,512]{1,0:T(8,128)S(1)}, f32[64,512]{1,0:T(8,128)S(1)}, u32[]{:S(2)}, u32[]{:S(2)}) %collective-permute-start.8) | collective-permute-done | bytes 131104 | tf_op jit(solution)/shard_map/ppermute | solution.py:380
  83.9 0.5 collective-permute-done.7.c_ref
  84.4 1.3 collective-permute-done.6.b_ref
  85.7 1.3 collective-permute-start.9
  87.0 1.9 %collective-permute-done.9.after_ref = f32[64,512]{1,0:T(8,128)S(1)} collective-permute-done((f32[64,512]{1,0:T(8,128)S(1)}, f32[64,512]{1,0:T(8,128)S(1)}, u32[]{:S(2)}, u32[]{:S(2)}) %collective-permute-start.9) | collective-permute-done | bytes 131104 | tf_op jit(solution)/shard_map/ppermute | solution.py:413
  89.1 3.4 %copy-done = bf16[512,8192]{1,0:T(8,128)(2,1)S(1)} copy-done((bf16[512,8192]{1,0:T(8,128)(2,1)S(1)}, bf16[512,8192]{1,0:T(8,128)(2,1)}, u32[]{:S(2)}) %copy-start) | copy-done | bytes 8388632
  92.4 2.0 %encode_other_half.1 = f32[8,8,4096]{2,1,0:T(8,128)S(1)} custom-call(s32[4]{0:T(128)S(1)} %copy-done.4, bf16[64,512]{1,0:T(8,128)(2,1)S(1)} %shard_map.99.hidden_ref, bf16[512,8192]{1,0:T(8,128)(2,1)S(1)} %copy-done), custom_call_target="tpu_custom_call" | custom-call | tf_op jit(solution)/shard_map/encode_other_half/pallas_call | solution.py:216
  94.5 4.5 %collective-permute-start.10 = (f32[8,8,4096]{2,1,0:T(8,128)S(1)}, f32[8,8,4096]{2,1,0:T(8,128)S(1)}, u32[]{:S(2)}, u32[]{:S(2)}) collective-permute-start(f32[8,8,4096]{2,1,0:T(8,128)S(1)} %encode_other_half.1), channel_id=1, source_target_pairs={{0,8},{8,0},{16,24},{24,16},{32,40},{40,32},{48,56},{56,48},{64,72... | collective-permute-start | bytes 3145736 | tf_op jit(solution)/shard_map/ppermute | solution.py:298
  98.9 2.0 %encode_own_half.1 = f32[8,8,4096]{2,1,0:T(8,128)S(1)} custom-call(s32[4]{0:T(128)S(1)} %copy-done.4, bf16[64,512]{1,0:T(8,128)(2,1)S(1)} %shard_map.99.hidden_ref, bf16[512,8192]{1,0:T(8,128)(2,1)S(1)} %copy-done), custom_call_target="tpu_custom_call" | custom-call | tf_op jit(solution)/shard_map/encode_own_half/pallas_call | solution.py:216
  101.0 0.1 fusion.28
  101.1 0.1 collective-permute-done.10
  101.3 0.1 fusion.27
  101.5 2.9 %collective-permute-start.24 = (f32[2,2,2,8,1280]{4,3,2,1,0:T(8,128)S(1)}, f32[2,2,2,8,1280]{4,3,2,1,0:T(8,128)S(1)}, u32[]{:S(2)}, u32[]{:S(2)}) collective-permute-start(f32[2,2,2,8,1280]{4,3,2,1,0:T(8,128)S(1)} %fusion.15), channel_id=1, source_target_pairs={{0,96},{8,104},{16,112},{24,120},{32,64},{40,72},{48,80},{56,88},{... | collective-permute-start | bytes 983048 | tf_op jit(solution)/shard_map/ppermute | solution.py:294
  104.4 0.2 collective-permute-start.12
  104.7 2.1 %collective-permute-start.18 = (f32[2,2,2,8,1408]{4,3,2,1,0:T(8,128)S(1)}, f32[2,2,2,8,1408]{4,3,2,1,0:T(8,128)S(1)}, u32[]{:S(2)}, u32[]{:S(2)}) collective-permute-start(f32[2,2,2,8,1408]{4,3,2,1,0:T(8,128)S(1)} %fusion.6), channel_id=1, source_target_pairs={{0,32},{8,40},{16,48},{24,56},{32,0},{40,8},{48,16},{56,24},{64,96... | collective-permute-start | bytes 1081352 | tf_op jit(solution)/shard_map/ppermute | solution.py:294
  106.8 5.9 %collective-permute-done.24 = f32[2,2,2,8,1280]{4,3,2,1,0:T(8,128)S(1)} collective-permute-done((f32[2,2,2,8,1280]{4,3,2,1,0:T(8,128)S(1)}, f32[2,2,2,8,1280]{4,3,2,1,0:T(8,128)S(1)}, u32[]{:S(2)}, u32[]{:S(2)}) %collective-permute-start.24) | collective-permute-done | bytes 327712 | tf_op jit(solution)/shard_map/ppermute | solution.py:294
  112.8 2.4 %collective-permute-start.25 = (f32[2,2,8,1280]{3,2,1,0:T(8,128)S(1)}, f32[2,2,8,1280]{3,2,1,0:T(8,128)S(1)}, u32[]{:S(2)}, u32[]{:S(2)}) collective-permute-start(f32[2,2,8,1280]{3,2,1,0:T(8,128)S(1)} %slice_bitcast_fusion.4), channel_id=1, source_target_pairs={{0,16},{8,24},{16,0},{24,8},{32,48},{40,56},{48,32},{56,40},{64,80... | collective-permute-start | bytes 491528 | tf_op jit(solution)/shard_map/ppermute | solution.py:294
  115.2 0.4 collective-permute-start.13
  115.7 2.0 %collective-permute-start.19 = (f32[2,2,8,1408]{3,2,1,0:T(8,128)S(1)}, f32[2,2,8,1408]{3,2,1,0:T(8,128)S(1)}, u32[]{:S(2)}, u32[]{:S(2)}) collective-permute-start(f32[2,2,8,1408]{3,2,1,0:T(8,128)S(1)} %slice_bitcast_fusion), channel_id=1, source_target_pairs={{0,96},{8,104},{16,112},{24,120},{32,64},{40,72},{48,80},{56,88},{... | collective-permute-start | bytes 540680 | tf_op jit(solution)/shard_map/ppermute | solution.py:294
  117.6 1.4 collective-permute-done.25
  119.1 0.4 collective-permute-start.26
  119.4 1.9 %collective-permute-done.13 = f32[2,2,8,1408]{3,2,1,0:T(8,128)S(1)} collective-permute-done((f32[2,2,8,1408]{3,2,1,0:T(8,128)S(1)}, f32[2,2,8,1408]{3,2,1,0:T(8,128)S(1)}, u32[]{:S(2)}, u32[]{:S(2)}) %collective-permute-start.13) | collective-permute-done | bytes 180256 | tf_op jit(solution)/shard_map/ppermute | solution.py:294
  121.3 0.7 collective-permute-start.14
  122.1 0.4 collective-permute-done.19
  122.5 1.8 %collective-permute-start.20 = (f32[2,8,1408]{2,1,0:T(8,128)S(1)}, f32[2,8,1408]{2,1,0:T(8,128)S(1)}, u32[]{:S(2)}, u32[]{:S(2)}) collective-permute-start(f32[2,8,1408]{2,1,0:T(8,128)S(1)} %slice_bitcast_fusion.6), channel_id=1, source_target_pairs={{0,16},{8,24},{16,0},{24,8},{32,48},{40,56},{48,32},{56,40},{64,80... | collective-permute-start | bytes 270344 | tf_op jit(solution)/shard_map/ppermute | solution.py:294
  124.4 2.8 %collective-permute-done.14 = f32[2,8,1408]{2,1,0:T(8,128)S(1)} collective-permute-done((f32[2,8,1408]{2,1,0:T(8,128)S(1)}, f32[2,8,1408]{2,1,0:T(8,128)S(1)}, u32[]{:S(2)}, u32[]{:S(2)}) %collective-permute-start.14) | collective-permute-done | bytes 90144 | tf_op jit(solution)/shard_map/ppermute | solution.py:294
  127.2 0.7 collective-permute-start.15
  127.9 2.0 %collective-permute-start.21 = (f32[2,8,1408]{2,1,0:T(8,128)S(1)}, f32[2,8,1408]{2,1,0:T(8,128)S(1)}, u32[]{:S(2)}, u32[]{:S(2)}) collective-permute-start(f32[2,8,1408]{2,1,0:T(8,128)S(1)} %fusion.21), channel_id=1, source_target_pairs={{0,16},{8,24},{16,0},{24,8},{32,48},{40,56},{48,32},{56,40},{64,80... | collective-permute-start | bytes 270344 | tf_op jit(solution)/shard_map/ppermute | solution.py:294
  130.0 0.2 collective-permute-start.28
  130.1 3.0 %collective-permute-done.15 = f32[2,8,1408]{2,1,0:T(8,128)S(1)} collective-permute-done((f32[2,8,1408]{2,1,0:T(8,128)S(1)}, f32[2,8,1408]{2,1,0:T(8,128)S(1)}, u32[]{:S(2)}, u32[]{:S(2)}) %collective-permute-start.15) | collective-permute-done | bytes 90144 | tf_op jit(solution)/shard_map/ppermute | solution.py:294
  133.3 1.9 %collective-permute-start.22 = (f32[2,2,8,1408]{3,2,1,0:T(8,128)S(1)}, f32[2,2,8,1408]{3,2,1,0:T(8,128)S(1)}, u32[]{:S(2)}, u32[]{:S(2)}) collective-permute-start(f32[2,2,8,1408]{3,2,1,0:T(8,128)S(1)} %get-tuple-element.37), channel_id=1, source_target_pairs={{0,96},{8,104},{16,112},{24,120},{32,64},{40,72},{48,80},{56,88},{... | collective-permute-start | bytes 540680 | tf_op jit(solution)/shard_map/ppermute | solution.py:294
  135.2 4.8 %collective-permute-done.16 = f32[2,2,8,1408]{3,2,1,0:T(8,128)S(1)} collective-permute-done((f32[2,2,8,1408]{3,2,1,0:T(8,128)S(1)}, f32[2,2,8,1408]{3,2,1,0:T(8,128)S(1)}, u32[]{:S(2)}, u32[]{:S(2)}) %collective-permute-start.16) | collective-permute-done | bytes 180256 | tf_op jit(solution)/shard_map/ppermute | solution.py:294
  140.2 0.8 collective-permute-start.32
  141.1 2.0 %collective-permute-start.34 = (f32[2,2,2,8,1280]{4,3,2,1,0:T(8,128)S(1)}, f32[2,2,2,8,1280]{4,3,2,1,0:T(8,128)S(1)}, u32[]{:S(2)}, u32[]{:S(2)}) collective-permute-start(f32[2,2,2,8,1280]{4,3,2,1,0:T(8,128)S(1)} %pad_maximum_fusion.5), channel_id=1, source_target_pairs={{0,96},{8,104},{16,112},{24,120},{32,64},{40,72},{48,80},{56,88},{... | collective-permute-start | bytes 983048 | tf_op jit(solution)/shard_map/ppermute | solution.py:294
  143.1 0.1 collective-permute-start.17
  143.2 0.4 collective-permute-start.23
  143.6 4.0 %collective-permute-done.30 = f32[2,2,2,8,1408]{4,3,2,1,0:T(8,128)S(1)} collective-permute-done((f32[2,2,2,8,1408]{4,3,2,1,0:T(8,128)S(1)}, f32[2,2,2,8,1408]{4,3,2,1,0:T(8,128)S(1)}, u32[]{:S(2)}, u32[]{:S(2)}) %collective-permute-start.30) | collective-permute-done | bytes 360480 | tf_op jit(solution)/shard_map/ppermute | solution.py:294
  147.6 0.1 collective-permute-done.32
  147.7 0.4 collective-permute-start.33
  148.1 4.3 %collective-permute-done.34 = f32[2,2,2,8,1280]{4,3,2,1,0:T(8,128)S(1)} collective-permute-done((f32[2,2,2,8,1280]{4,3,2,1,0:T(8,128)S(1)}, f32[2,2,2,8,1280]{4,3,2,1,0:T(8,128)S(1)}, u32[]{:S(2)}, u32[]{:S(2)}) %collective-permute-start.34) | collective-permute-done | bytes 327712 | tf_op jit(solution)/shard_map/ppermute | solution.py:294
  152.5 2.3 %assemble.1 = (f32[64,8192]{1,0:T(8,128)}, f32[64,8192]{1,0:T(8,128)}) custom-call(s32[4]{0:T(128)S(1)} %copy-done.4, f32[4,2,8,1408]{3,2,1,0:T(8,128)S(1)} %bitcast.110, f32[4,2,8,1408]{3,2,1,0:T(8,128)S(1)} %collective-permute-done.17.refs_1_, f32[4,2,8,1408]{3,2,1,0:T(8,128)S(1)} %bitcast.112, f32[4,2,8,1408]{3,2,1,0:T(8,128)S(1)} %collective-permute-done.23.refs_3_, ...), custom_call_target="tpu_custom_call" | custom-call | tf_op jit(solution)/shard_map/assemble/pallas_call | solution.py:264
  154.8 2.3 %assemble_rest.1 = (f32[64,8192]{1,0:T(8,128)}, f32[64,8192]{1,0:T(8,128)}) custom-call(s32[4]{0:T(128)S(1)} %copy-done.4, f32[64,8192]{1,0:T(8,128)} %get-tuple-element.28.refs_0_, f32[64,8192]{1,0:T(8,128)} %get-tuple-element.29.refs_1_, f32[4,2,8,1408]{3,2,1,0:T(8,128)S(1)} %bitcast.116, ...), custom_call_target="tpu_custom_call", output_to_operand_aliasing={{0}: (1, {}), {1}: (2, {})} | custom-call | tf_op jit(solution)/shard_map/assemble_rest/pallas_call | solution.py:264
  (65 shorter events, 1.4 us)
Async XLA Ops:
  0.6 45.1 %copy-start.7 = (f32[64]{0:T(128)S(1)}, f32[64]{0:T(128)}, u32[]{:S(2)}) copy-start(f32[64]{0:T(128)} %param.12) | copy-start | bytes 772
  31.7 7.0 %collective-permute-start = (f32[64,512]{1,0:T(8,128)}, f32[64,512]{1,0:T(8,128)S(1)}, u32[]{:S(2)}, u32[]{:S(2)}) collective-permute-start(f32[64,512]{1,0:T(8,128)} %get-tuple-element.19.a_ref), channel_id=1, source_target_pairs={{0,4},{1,5},{2,6},{3,7},{4,0},{5,1},{6,2},{7,3},{8,12},{9,13},{10,... | collective-permute-start | bytes 393224 | tf_op jit(solution)/shard_map/ppermute | solution.py:375
  38.7 0.9 copy-start.2
  39.7 7.5 %collective-permute-start.3 = (f32[64,512]{1,0:T(8,128)S(1)}, f32[64,512]{1,0:T(8,128)S(1)}, u32[]{:S(2)}, u32[]{:S(2)}) collective-permute-start(f32[64,512]{1,0:T(8,128)S(1)} %shard_map.95.a_ref), channel_id=1, source_target_pairs={{0,2},{1,3},{2,0},{3,1},{4,6},{5,7},{6,4},{7,5},{8,10},{9,11},{10,... | collective-permute-start | bytes 393224 | tf_op jit(solution)/shard_map/ppermute | solution.py:380
  43.7 6.2 %collective-permute-start.2 = (f32[64,512]{1,0:T(8,128)S(1)}, f32[64,512]{1,0:T(8,128)S(1)}, u32[]{:S(2)}, u32[]{:S(2)}) collective-permute-start(f32[64,512]{1,0:T(8,128)S(1)} %shard_map.95.a_ref), channel_id=1, source_target_pairs={{0,3},{1,0},{2,1},{3,2},{4,7},{5,4},{6,5},{7,6},{8,11},{9,8},{10,9... | collective-permute-start | bytes 393224 | tf_op jit(solution)/shard_map/ppermute | solution.py:380
  44.4 6.2 %collective-permute-start.1 = (f32[64,512]{1,0:T(8,128)S(1)}, f32[64,512]{1,0:T(8,128)S(1)}, u32[]{:S(2)}, u32[]{:S(2)}) collective-permute-start(f32[64,512]{1,0:T(8,128)S(1)} %shard_map.95.a_ref), channel_id=1, source_target_pairs={{0,1},{1,2},{2,3},{3,0},{4,5},{5,6},{6,7},{7,4},{8,9},{9,10},{10,1... | collective-permute-start | bytes 393224 | tf_op jit(solution)/shard_map/ppermute | solution.py:380
  50.7 2.2 %copy-start.3 = (bf16[64,512]{1,0:T(8,128)(2,1)}, bf16[64,512]{1,0:T(8,128)(2,1)S(1)}, u32[]{:S(2)}) copy-start(bf16[64,512]{1,0:T(8,128)(2,1)S(1)} %get-tuple-element.21.latent_ref) | copy-start | bytes 196612
  50.7 2.2 %collective-permute-start.4 = (bf16[64,512]{1,0:T(8,128)(2,1)S(1)}, bf16[64,512]{1,0:T(8,128)(2,1)S(1)}, u32[]{:S(2)}, u32[]{:S(2)}) collective-permute-start(bf16[64,512]{1,0:T(8,128)(2,1)S(1)} %get-tuple-element.21.latent_ref), channel_id=1, source_target_pairs={{0,8},{8,16},{16,24},{24,32},{32,40},{40,48},{48,56},{56,64},{64,7... | collective-permute-start | bytes 196616 | tf_op jit(solution)/shard_map/ppermute | solution.py:407
  52.9 0.6 copy-start.6
  53.5 35.6 %copy-start.4 = (s32[4]{0:T(128)S(1)}, s32[4]{0:T(128)}, u32[]{:S(2)}) copy-start(s32[4]{0:T(128)} %pad_add_fusion.info_ref) | copy-start | bytes 52
  65.1 35.8 %collective-permute-start.11 = (f32[8,8,4096]{2,1,0:T(8,128)}, f32[8,8,4096]{2,1,0:T(8,128)S(1)}, u32[]{:S(2)}, u32[]{:S(2)}) collective-permute-start(f32[8,8,4096]{2,1,0:T(8,128)} %get-tuple-element.27), channel_id=1, source_target_pairs={{0,8},{8,0},{16,24},{24,16},{32,40},{40,32},{48,56},{56,48},{64,72... | collective-permute-start | bytes 3145736 | tf_op jit(solution)/shard_map/ppermute | solution.py:298
  68.0 7.2 %collective-permute-start.5 = (f32[64,512]{1,0:T(8,128)}, f32[64,512]{1,0:T(8,128)S(1)}, u32[]{:S(2)}, u32[]{:S(2)}) collective-permute-start(f32[64,512]{1,0:T(8,128)} %get-tuple-element.23.a_ref), channel_id=1, source_target_pairs={{0,4},{1,5},{2,6},{3,7},{4,0},{5,1},{6,2},{7,3},{8,12},{9,13},{10,... | collective-permute-start | bytes 393224 | tf_op jit(solution)/shard_map/ppermute | solution.py:375
  75.2 0.9 copy-start.1
  76.1 7.8 %collective-permute-start.8 = (f32[64,512]{1,0:T(8,128)S(1)}, f32[64,512]{1,0:T(8,128)S(1)}, u32[]{:S(2)}, u32[]{:S(2)}) collective-permute-start(f32[64,512]{1,0:T(8,128)S(1)} %shard_map.97.a_ref), channel_id=1, source_target_pairs={{0,2},{1,3},{2,0},{3,1},{4,6},{5,7},{6,4},{7,5},{8,10},{9,11},{10,... | collective-permute-start | bytes 393224 | tf_op jit(solution)/shard_map/ppermute | solution.py:380
  78.0 6.4 %collective-permute-start.7 = (f32[64,512]{1,0:T(8,128)S(1)}, f32[64,512]{1,0:T(8,128)S(1)}, u32[]{:S(2)}, u32[]{:S(2)}) collective-permute-start(f32[64,512]{1,0:T(8,128)S(1)} %shard_map.97.a_ref), channel_id=1, source_target_pairs={{0,3},{1,0},{2,1},{3,2},{4,7},{5,4},{6,5},{7,6},{8,11},{9,8},{10,9... | collective-permute-start | bytes 393224 | tf_op jit(solution)/shard_map/ppermute | solution.py:380
  79.2 6.5 %collective-permute-start.6 = (f32[64,512]{1,0:T(8,128)S(1)}, f32[64,512]{1,0:T(8,128)S(1)}, u32[]{:S(2)}, u32[]{:S(2)}) collective-permute-start(f32[64,512]{1,0:T(8,128)S(1)} %shard_map.97.a_ref), channel_id=1, source_target_pairs={{0,1},{1,2},{2,3},{3,0},{4,5},{5,6},{6,7},{7,4},{8,9},{9,10},{10,1... | collective-permute-start | bytes 393224 | tf_op jit(solution)/shard_map/ppermute | solution.py:380
  85.7 3.2 %collective-permute-start.9 = (f32[64,512]{1,0:T(8,128)S(1)}, f32[64,512]{1,0:T(8,128)S(1)}, u32[]{:S(2)}, u32[]{:S(2)}) collective-permute-start(f32[64,512]{1,0:T(8,128)S(1)} %shard_map.98.back_ref), channel_id=1, source_target_pairs={{8,0},{16,8},{24,16},{32,24},{40,32},{48,40},{56,48},{64,56},{72,6... | collective-permute-start | bytes 393224 | tf_op jit(solution)/shard_map/ppermute | solution.py:413
  89.1 3.4 %copy-start = (bf16[512,8192]{1,0:T(8,128)(2,1)S(1)}, bf16[512,8192]{1,0:T(8,128)(2,1)}, u32[]{:S(2)}) copy-start(bf16[512,8192]{1,0:T(8,128)(2,1)} %get-tuple-element.22.contact_ref) | copy-start | bytes 25165828
  94.5 6.5 %copy-start.5 = (f32[8,8,4096]{2,1,0:T(8,128)S(1)}, f32[8,8,4096]{2,1,0:T(8,128)}, u32[]{:S(2)}) copy-start(f32[8,8,4096]{2,1,0:T(8,128)} %get-tuple-element.26) | copy-start | bytes 3145732
  94.5 6.8 %collective-permute-start.10 = (f32[8,8,4096]{2,1,0:T(8,128)S(1)}, f32[8,8,4096]{2,1,0:T(8,128)S(1)}, u32[]{:S(2)}, u32[]{:S(2)}) collective-permute-start(f32[8,8,4096]{2,1,0:T(8,128)S(1)} %encode_other_half.1), channel_id=1, source_target_pairs={{0,8},{8,0},{16,24},{24,16},{32,40},{40,32},{48,56},{56,48},{64,72... | collective-permute-start | bytes 3145736 | tf_op jit(solution)/shard_map/ppermute | solution.py:298
  101.5 11.3 %collective-permute-start.24 = (f32[2,2,2,8,1280]{4,3,2,1,0:T(8,128)S(1)}, f32[2,2,2,8,1280]{4,3,2,1,0:T(8,128)S(1)}, u32[]{:S(2)}, u32[]{:S(2)}) collective-permute-start(f32[2,2,2,8,1280]{4,3,2,1,0:T(8,128)S(1)} %fusion.15), channel_id=1, source_target_pairs={{0,96},{8,104},{16,112},{24,120},{32,64},{40,72},{48,80},{56,88},{... | collective-permute-start | bytes 983048 | tf_op jit(solution)/shard_map/ppermute | solution.py:294
  104.4 10.8 %collective-permute-start.12 = (f32[2,2,2,8,1408]{4,3,2,1,0:T(8,128)S(1)}, f32[2,2,2,8,1408]{4,3,2,1,0:T(8,128)S(1)}, u32[]{:S(2)}, u32[]{:S(2)}) collective-permute-start(f32[2,2,2,8,1408]{4,3,2,1,0:T(8,128)S(1)} %fusion.7), channel_id=1, source_target_pairs={{0,16},{8,24},{16,0},{24,8},{32,48},{40,56},{48,32},{56,40},{64,80... | collective-permute-start | bytes 1081352 | tf_op jit(solution)/shard_map/ppermute | solution.py:294
  104.7 10.9 %collective-permute-start.18 = (f32[2,2,2,8,1408]{4,3,2,1,0:T(8,128)S(1)}, f32[2,2,2,8,1408]{4,3,2,1,0:T(8,128)S(1)}, u32[]{:S(2)}, u32[]{:S(2)}) collective-permute-start(f32[2,2,2,8,1408]{4,3,2,1,0:T(8,128)S(1)} %fusion.6), channel_id=1, source_target_pairs={{0,32},{8,40},{16,48},{24,56},{32,0},{40,8},{48,16},{56,24},{64,96... | collective-permute-start | bytes 1081352 | tf_op jit(solution)/shard_map/ppermute | solution.py:294
  112.8 6.2 %collective-permute-start.25 = (f32[2,2,8,1280]{3,2,1,0:T(8,128)S(1)}, f32[2,2,8,1280]{3,2,1,0:T(8,128)S(1)}, u32[]{:S(2)}, u32[]{:S(2)}) collective-permute-start(f32[2,2,8,1280]{3,2,1,0:T(8,128)S(1)} %slice_bitcast_fusion.4), channel_id=1, source_target_pairs={{0,16},{8,24},{16,0},{24,8},{32,48},{40,56},{48,32},{56,40},{64,80... | collective-permute-start | bytes 491528 | tf_op jit(solution)/shard_map/ppermute | solution.py:294
  115.2 6.1 %collective-permute-start.13 = (f32[2,2,8,1408]{3,2,1,0:T(8,128)S(1)}, f32[2,2,8,1408]{3,2,1,0:T(8,128)S(1)}, u32[]{:S(2)}, u32[]{:S(2)}) collective-permute-start(f32[2,2,8,1408]{3,2,1,0:T(8,128)S(1)} %slice_bitcast_fusion.2), channel_id=1, source_target_pairs={{0,32},{8,40},{16,48},{24,56},{32,0},{40,8},{48,16},{56,24},{64,96... | collective-permute-start | bytes 540680 | tf_op jit(solution)/shard_map/ppermute | solution.py:294
  115.7 6.8 %collective-permute-start.19 = (f32[2,2,8,1408]{3,2,1,0:T(8,128)S(1)}, f32[2,2,8,1408]{3,2,1,0:T(8,128)S(1)}, u32[]{:S(2)}, u32[]{:S(2)}) collective-permute-start(f32[2,2,8,1408]{3,2,1,0:T(8,128)S(1)} %slice_bitcast_fusion), channel_id=1, source_target_pairs={{0,96},{8,104},{16,112},{24,120},{32,64},{40,72},{48,80},{56,88},{... | collective-permute-start | bytes 540680 | tf_op jit(solution)/shard_map/ppermute | solution.py:294
  119.1 5.2 %collective-permute-start.26 = (f32[2,8,1280]{2,1,0:T(8,128)S(1)}, f32[2,8,1280]{2,1,0:T(8,128)S(1)}, u32[]{:S(2)}, u32[]{:S(2)}) collective-permute-start(f32[2,8,1280]{2,1,0:T(8,128)S(1)} %slice_bitcast_fusion.10), channel_id=1, source_target_pairs={{0,32},{8,40},{16,48},{24,56},{32,0},{40,8},{48,16},{56,24},{64,96... | collective-permute-start | bytes 245768 | tf_op jit(solution)/shard_map/ppermute | solution.py:294
  121.3 5.8 %collective-permute-start.14 = (f32[2,8,1408]{2,1,0:T(8,128)S(1)}, f32[2,8,1408]{2,1,0:T(8,128)S(1)}, u32[]{:S(2)}, u32[]{:S(2)}) collective-permute-start(f32[2,8,1408]{2,1,0:T(8,128)S(1)} %slice_bitcast_fusion.8), channel_id=1, source_target_pairs={{0,96},{8,104},{16,112},{24,120},{32,64},{40,72},{48,80},{56,88},{... | collective-permute-start | bytes 270344 | tf_op jit(solution)/shard_map/ppermute | solution.py:294
  122.5 5.4 %collective-permute-start.20 = (f32[2,8,1408]{2,1,0:T(8,128)S(1)}, f32[2,8,1408]{2,1,0:T(8,128)S(1)}, u32[]{:S(2)}, u32[]{:S(2)}) collective-permute-start(f32[2,8,1408]{2,1,0:T(8,128)S(1)} %slice_bitcast_fusion.6), channel_id=1, source_target_pairs={{0,16},{8,24},{16,0},{24,8},{32,48},{40,56},{48,32},{56,40},{64,80... | collective-permute-start | bytes 270344 | tf_op jit(solution)/shard_map/ppermute | solution.py:294
  124.3 5.6 %collective-permute-start.27 = (f32[2,8,1280]{2,1,0:T(8,128)S(1)}, f32[2,8,1280]{2,1,0:T(8,128)S(1)}, u32[]{:S(2)}, u32[]{:S(2)}) collective-permute-start(f32[2,8,1280]{2,1,0:T(8,128)S(1)} %fusion.23), channel_id=1, source_target_pairs={{0,32},{8,40},{16,48},{24,56},{32,0},{40,8},{48,16},{56,24},{64,96... | collective-permute-start | bytes 245768 | tf_op jit(solution)/shard_map/ppermute | solution.py:294
  127.2 6.0 %collective-permute-start.15 = (f32[2,8,1408]{2,1,0:T(8,128)S(1)}, f32[2,8,1408]{2,1,0:T(8,128)S(1)}, u32[]{:S(2)}, u32[]{:S(2)}) collective-permute-start(f32[2,8,1408]{2,1,0:T(8,128)S(1)} %fusion.22), channel_id=1, source_target_pairs={{0,96},{8,104},{16,112},{24,120},{32,64},{40,72},{48,80},{56,88},{... | collective-permute-start | bytes 270344 | tf_op jit(solution)/shard_map/ppermute | solution.py:294
  127.9 5.4 %collective-permute-start.21 = (f32[2,8,1408]{2,1,0:T(8,128)S(1)}, f32[2,8,1408]{2,1,0:T(8,128)S(1)}, u32[]{:S(2)}, u32[]{:S(2)}) collective-permute-start(f32[2,8,1408]{2,1,0:T(8,128)S(1)} %fusion.21), channel_id=1, source_target_pairs={{0,16},{8,24},{16,0},{24,8},{32,48},{40,56},{48,32},{56,40},{64,80... | collective-permute-start | bytes 270344 | tf_op jit(solution)/shard_map/ppermute | solution.py:294
  130.0 11.0 %collective-permute-start.28 = (f32[2,2,8,1280]{3,2,1,0:T(8,128)S(1)}, f32[2,2,8,1280]{3,2,1,0:T(8,128)S(1)}, u32[]{:S(2)}, u32[]{:S(2)}) collective-permute-start(f32[2,2,8,1280]{3,2,1,0:T(8,128)S(1)} %get-tuple-element.41), channel_id=1, source_target_pairs={{0,16},{8,24},{16,0},{24,8},{32,48},{40,56},{48,32},{56,40},{64,80... | collective-permute-start | bytes 491528 | tf_op jit(solution)/shard_map/ppermute | solution.py:294
  133.2 6.9 %collective-permute-start.16 = (f32[2,2,8,1408]{3,2,1,0:T(8,128)S(1)}, f32[2,2,8,1408]{3,2,1,0:T(8,128)S(1)}, u32[]{:S(2)}, u32[]{:S(2)}) collective-permute-start(f32[2,2,8,1408]{3,2,1,0:T(8,128)S(1)} %get-tuple-element.39), channel_id=1, source_target_pairs={{0,32},{8,40},{16,48},{24,56},{32,0},{40,8},{48,16},{56,24},{64,96... | collective-permute-start | bytes 540680 | tf_op jit(solution)/shard_map/ppermute | solution.py:294
  133.3 6.9 %collective-permute-start.22 = (f32[2,2,8,1408]{3,2,1,0:T(8,128)S(1)}, f32[2,2,8,1408]{3,2,1,0:T(8,128)S(1)}, u32[]{:S(2)}, u32[]{:S(2)}) collective-permute-start(f32[2,2,8,1408]{3,2,1,0:T(8,128)S(1)} %get-tuple-element.37), channel_id=1, source_target_pairs={{0,96},{8,104},{16,112},{24,120},{32,64},{40,72},{48,80},{56,88},{... | collective-permute-start | bytes 540680 | tf_op jit(solution)/shard_map/ppermute | solution.py:294
  140.1 7.5 %collective-permute-start.30 = (f32[2,2,2,8,1408]{4,3,2,1,0:T(8,128)S(1)}, f32[2,2,2,8,1408]{4,3,2,1,0:T(8,128)S(1)}, u32[]{:S(2)}, u32[]{:S(2)}) collective-permute-start(f32[2,2,2,8,1408]{4,3,2,1,0:T(8,128)S(1)} %pad_maximum_fusion.2), channel_id=1, source_target_pairs={{0,16},{8,24},{16,0},{24,8},{32,48},{40,56},{48,32},{56,40},{64,80... | collective-permute-start | bytes 1081352 | tf_op jit(solution)/shard_map/ppermute | solution.py:294
  140.2 7.5 %collective-permute-start.32 = (f32[2,2,2,8,1408]{4,3,2,1,0:T(8,128)S(1)}, f32[2,2,2,8,1408]{4,3,2,1,0:T(8,128)S(1)}, u32[]{:S(2)}, u32[]{:S(2)}) collective-permute-start(f32[2,2,2,8,1408]{4,3,2,1,0:T(8,128)S(1)} %pad_maximum_fusion.3), channel_id=1, source_target_pairs={{0,32},{8,40},{16,48},{24,56},{32,0},{40,8},{48,16},{56,24},{64,96... | collective-permute-start | bytes 1081352 | tf_op jit(solution)/shard_map/ppermute | solution.py:294
  141.0 2.2 %collective-permute-start.29 = (f32[4,2,8,1280]{3,2,1,0:T(8,128)S(1)}, f32[4,2,8,1280]{3,2,1,0:T(8,128)S(1)}, u32[]{:S(2)}, u32[]{:S(2)}) collective-permute-start(f32[4,2,8,1280]{3,2,1,0:T(8,128)S(1)} %bitcast.113), channel_id=1, source_target_pairs={{0,8},{8,0},{16,24},{24,16},{32,40},{40,32},{48,56},{56,48},{64,72... | collective-permute-start | bytes 983048 | tf_op jit(solution)/shard_map/ppermute | solution.py:298
  141.1 11.3 %collective-permute-start.34 = (f32[2,2,2,8,1280]{4,3,2,1,0:T(8,128)S(1)}, f32[2,2,2,8,1280]{4,3,2,1,0:T(8,128)S(1)}, u32[]{:S(2)}, u32[]{:S(2)}) collective-permute-start(f32[2,2,2,8,1280]{4,3,2,1,0:T(8,128)S(1)} %pad_maximum_fusion.5), channel_id=1, source_target_pairs={{0,96},{8,104},{16,112},{24,120},{32,64},{40,72},{48,80},{56,88},{... | collective-permute-start | bytes 983048 | tf_op jit(solution)/shard_map/ppermute | solution.py:294
  143.1 9.4 %collective-permute-start.17 = (f32[4,2,8,1408]{3,2,1,0:T(8,128)S(1)}, f32[4,2,8,1408]{3,2,1,0:T(8,128)S(1)}, u32[]{:S(2)}, u32[]{:S(2)}) collective-permute-start(f32[4,2,8,1408]{3,2,1,0:T(8,128)S(1)} %bitcast.109), channel_id=1, source_target_pairs={{0,8},{8,0},{16,24},{24,16},{32,40},{40,32},{48,56},{56,48},{64,72... | collective-permute-start | bytes 1081352 | tf_op jit(solution)/shard_map/ppermute | solution.py:298
  143.2 9.2 %collective-permute-start.23 = (f32[4,2,8,1408]{3,2,1,0:T(8,128)S(1)}, f32[4,2,8,1408]{3,2,1,0:T(8,128)S(1)}, u32[]{:S(2)}, u32[]{:S(2)}) collective-permute-start(f32[4,2,8,1408]{3,2,1,0:T(8,128)S(1)} %bitcast.111), channel_id=1, source_target_pairs={{0,8},{8,0},{16,24},{24,16},{32,40},{40,32},{48,56},{56,48},{64,72... | collective-permute-start | bytes 1081352 | tf_op jit(solution)/shard_map/ppermute | solution.py:298
  147.6 7.1 %collective-permute-start.31 = (f32[4,2,8,1408]{3,2,1,0:T(8,128)S(1)}, f32[4,2,8,1408]{3,2,1,0:T(8,128)S(1)}, u32[]{:S(2)}, u32[]{:S(2)}) collective-permute-start(f32[4,2,8,1408]{3,2,1,0:T(8,128)S(1)} %bitcast.115), channel_id=1, source_target_pairs={{0,8},{8,0},{16,24},{24,16},{32,40},{40,32},{48,56},{56,48},{64,72... | collective-permute-start | bytes 1081352 | tf_op jit(solution)/shard_map/ppermute | solution.py:298
  147.7 7.0 %collective-permute-start.33 = (f32[4,2,8,1408]{3,2,1,0:T(8,128)S(1)}, f32[4,2,8,1408]{3,2,1,0:T(8,128)S(1)}, u32[]{:S(2)}, u32[]{:S(2)}) collective-permute-start(f32[4,2,8,1408]{3,2,1,0:T(8,128)S(1)} %bitcast.117), channel_id=1, source_target_pairs={{0,8},{8,0},{16,24},{24,16},{32,40},{40,32},{48,56},{56,48},{64,72... | collective-permute-start | bytes 1081352 | tf_op jit(solution)/shard_map/ppermute | solution.py:298
  152.5 2.3 %collective-permute-start.35 = (f32[4,2,8,1280]{3,2,1,0:T(8,128)S(1)}, f32[4,2,8,1280]{3,2,1,0:T(8,128)S(1)}, u32[]{:S(2)}, u32[]{:S(2)}) collective-permute-start(f32[4,2,8,1280]{3,2,1,0:T(8,128)S(1)} %bitcast.119), channel_id=1, source_target_pairs={{0,8},{8,0},{16,24},{24,16},{32,40},{40,32},{48,56},{56,48},{64,72... | collective-permute-start | bytes 983048 | tf_op jit(solution)/shard_map/ppermute | solution.py:298
where the time goes:
time: 159 us; the launch traced here: 157 us
  Pallas kernels  50.1 us (32%)
  waiting for transfers between devices  50.1 us (32%)
  starting transfers between devices  47.6 us (30%)
  local copies, waits for them, and re-layouts  5.97 us (4%)
  between operations  1.9 us (1%)
    pallas_call x1, Pallas kernels, contacts_and_sum(): pl.pallas_call(contact_kernel, grid_spec=pltpu.PrefetchScalarGridSpec(num...  29.7 us
    ppermute x18, waiting for transfers between devices, flip(): return lax.ppermute(value, 'frames', route)  28.7 us
    ppermute x18, starting transfers between devices, flip(): return lax.ppermute(value, 'frames', route)  20.6 us
    pallas_call x1, Pallas kernels, decode(): pl.pallas_call(decode_kernel, grid_spec=pltpu.PrefetchScalarGridSpec(num_...  11.7 us
    ppermute x6, waiting for transfers between devices, terms_over_pairs(): terms.append(lax.ppermute(value, 'pairs', route))  10.5 us
    ppermute x6, starting transfers between devices, terms_over_pairs(): terms.append(lax.ppermute(value, 'pairs', route))  9.93 us
    ppermute x8, starting transfers between devices, swap_cores(): return lax.ppermute(value, 'frames', [(i, i ^ 1) for i in range(16)])  8.27 us
    ppermute x2, waiting for transfers between devices, terms_over_pairs(): got = lax.ppermute(value, 'pairs', [(i, i ^ 4) for i in range(8)])  8.01 us
  transfers between devices with their start and end apart: 36, of which 21 were waited for; matrix products, arithmetic and copies ran while one was open for 0% of the time, Pallas kernels for 4%

commit v1 on v0

--- a/solution.py
+++ b/solution.py
@@ -21,7 +21,7 @@
 
 
 scaling = 1.0 / (softness * math.log(2.0))
-CHUNK = 64
+CHUNK = 16
 
 
 def contact_kernel(first_ref, second_ref, coords_ref, enc_ref, contact_ref, sum_ref, table, total):
@@ -97,7 +97,7 @@
             jax.ShapeDtypeStruct((frames, pairs), BF),
             jax.ShapeDtypeStruct((latents, frames), F32),
         ],
-        compiler_params=params(56),
+        compiler_params=params(42),
         name="contacts",
     )(first, second.reshape(1, pairs), coords, enc)
 
@@ -199,7 +199,7 @@
             jax.ShapeDtypeStruct((GROUPS, 8, pairs // 2), F32),
             jax.ShapeDtypeStruct((latents, frames), F32),
         ],
-        compiler_params=params(56),
+        compiler_params=params(36),
         name="decode",
     )(info, scale, latent, before, dec, bias.reshape(1, pairs), contact)
 
@@ -353,32 +353,43 @@
     out_ref[...] = a_ref[...] + b_ref[...]
 
 
-def add_four_kernel(a_ref, b_ref, c_ref, d_ref, out_ref):
-    out_ref[...] = (a_ref[...] + b_ref[...]) + (c_ref[...] + d_ref[...])
+def select_add_kernel(a_ref, b_ref, c_ref, d_ref, last_ref, out_ref):
+    frame = lax.broadcasted_iota(jnp.int32, out_ref.shape, 1)
+    own, after = a_ref[...] + b_ref[...], c_ref[...] + d_ref[...]
+    out_ref[...] = jnp.where(frame < last_ref[...], own, after)
 
 
 def latent_kernel(a_ref, b_ref, c_ref, d_ref, bias_ref, latent_ref, rounded_ref):
     total = (a_ref[...] + b_ref[...]) + (c_ref[...] + d_ref[...])
-    latent = jnp.tanh(total + bias_ref[...])
+    latents = total.shape[0]
+    row, column = (lax.broadcasted_iota(jnp.int32, (latents, latents), n) for n in (0, 1))
+    bias = jnp.sum(jnp.where(row == column, bias_ref[...], 0.0), axis=1, keepdims=True)
+    latent = jnp.tanh(total + bias)
     latent_ref[...] = latent
     rounded_ref[...] = latent.astype(BF)
 
 
-def hidden_kernel(back_ref, after_ref, latent_ref, last_ref, hidden_ref):
-    frame = lax.broadcasted_iota(jnp.int32, back_ref.shape, 1)
-    backward = jnp.where(frame < last_ref[...], back_ref[...], after_ref[...])
+def hidden_kernel(a_ref, b_ref, c_ref, d_ref, latent_ref, hidden_ref):
+    backward = (a_ref[...] + b_ref[...]) + (c_ref[...] + d_ref[...])
     latent = latent_ref[...]
     hidden_ref[...] = (backward * (1.0 - latent * latent)).astype(BF)
 
 
-def terms_over_pairs(value):
-    got = lax.ppermute(value, "pairs", [(i, i ^ 4) for i in range(8)])
-    (value,) = small_call(add_kernel, [(value.shape, F32)], value, got)
+def along_y(value):
+    return lax.ppermute(value, "pairs", [(i, i ^ 4) for i in range(8)])
+
+
+def along_z(value):
     terms = [value]
     for k in (1, 3, 2):
         route = [(i, (i // 4) * 4 + (i + k) % 4) for i in range(8)]
         terms.append(lax.ppermute(value, "pairs", route))
     return terms
+
+
+def from_next(value, flip_y):
+    route = [(f * 8 + (p ^ flip_y), (f - 1) * 8 + p) for f in range(1, 16) for p in range(8)]
+    return lax.ppermute(value, ("frames", "pairs"), route)
 
 
 def local(coords, pair_first, pair_second, enc_weight, enc_bias, dec_weight, dec_bias, lag_frames):
@@ -390,7 +401,7 @@
     info = jnp.stack([lag, (place == 0).astype(jnp.int32), place % 2, chip_code(place)])
     info = info.astype(jnp.int32)
     scale = (1.0 / jnp.sqrt(jnp.float32(total_frames) - lag.astype(F32))).reshape(1)
-    bias = enc_bias[:, None]
+    bias = enc_bias.reshape(1, -1)
     last = (frame_rows - lag).reshape(1, 1)
     pair_first, info, scale, bias, last = lax.optimization_barrier(
         (pair_first, info, scale, bias, last)
@@ -400,18 +411,22 @@
         jnp.transpose(coords, (1, 0, 2)), pair_first, pair_second, enc_weight, 2048
     )
     whole = partial_sum.shape
+    (half_sum,) = small_call(add_kernel, [(whole, F32)], partial_sum, along_y(partial_sum))
     latent, latent_bf = small_call(
         latent_kernel, [(whole, F32), (whole, BF)],
-        *terms_over_pairs(partial_sum), bias,
+        *along_z(half_sum), bias,
     )
     before = lax.ppermute(latent_bf, "frames", [(i, i + 1) for i in range(devices - 1)])
     dec_keep, give, back_terms = decode(
         info, scale, latent_bf, before, dec_weight, dec_bias, contact, 4
     )
     dec_got = swap_cores(give)
-    (rolled_back,) = small_call(add_four_kernel, [(whole, F32)], *terms_over_pairs(back_terms))
-    after = lax.ppermute(rolled_back, "frames", [(i + 1, i) for i in range(devices - 1)])
-    (hidden_bf,) = small_call(hidden_kernel, [(whole, BF)], rolled_back, after, latent, last)
+    (half_sum,) = small_call(
+        select_add_kernel, [(whole, F32)],
+        back_terms, along_y(back_terms),
+        from_next(back_terms, 0), from_next(back_terms, 4), last,
+    )
+    (hidden_bf,) = small_call(hidden_kernel, [(whole, BF)], *along_z(half_sum), latent)
     give = encode(info, hidden_bf, contact, 2, True)
     got = swap_cores(give)
     keep = encode(info, hidden_bf, contact, 2, False)

time: 159 us -> 153 us (0.962)
  Pallas kernels: 50.1 us -> 44.7 us
  waiting for transfers between devices: 50.1 us -> 52.6 us
    ppermute x8, starting transfers between devices: 8.27 us -> 3.94 us  [swap_cores(): return lax.ppermute(value, 'frames', [(i, i ^ 1) for i in range(16)])]
    ppermute x18, waiting for transfers between devices: 28.7 us -> 32.2 us  [flip(): return lax.ppermute(value, 'frames', route)]
    pallas_call x1, Pallas kernels: 29.7 us -> 26.5 us  [contacts_and_sum(): pl.pallas_call(contact_kernel, grid_spec=pltpu.PrefetchScalarGridSpec(num...]
    pallas_call x1, Pallas kernels: 11.7 us -> 9.44 us  [decode(): pl.pallas_call(decode_kernel, grid_spec=pltpu.PrefetchScalarGridSpec(num_...]
    ppermute x18, starting transfers between devices: 20.6 us -> 22.4 us  [flip(): return lax.ppermute(value, 'frames', route)]
    unnamed x16 -> x14, local copies, waits for them, and re-layouts: 5.82 us -> 4.31 us
    ppermute x9 -> x10, starting transfers between devices: 17.4 us -> 18.9 us  [the longest x6 9.94 us: along_z(): terms.append(lax.ppermute(value, 'pairs', route))]
    ppermute x9 -> x10, waiting for transfers between devices: 20.4 us -> 19.2 us  [the longest x6 12 us: along_z(): terms.append(lax.ppermute(value, 'pairs', route))]
  transfers between devices with their start and end apart: 36 -> 37, of which waited for: 21 -> 26; matrix products, arithmetic and copies ran while one was open for 0% -> 0% of each run, Pallas kernels for 4% -> 4%
where the time goes in v1:
time: 153 us; the launch traced here: 151 us
  waiting for transfers between devices  52.6 us (34%)
  starting transfers between devices  46.6 us (30%)
  Pallas kernels  44.7 us (29%)
  local copies, waits for them, and re-layouts  4.38 us (3%)
  between operations  1.88 us (1%)
    ppermute x18, waiting for transfers between devices, flip(): return lax.ppermute(value, 'frames', route)  32.2 us
    pallas_call x1, Pallas kernels, contacts_and_sum(): pl.pallas_call(contact_kernel, grid_spec=pltpu.PrefetchScalarGridSpec(num...  26.5 us
    ppermute x18, starting transfers between devices, flip(): return lax.ppermute(value, 'frames', route)  22.4 us
    ppermute x6, waiting for transfers between devices, along_z(): terms.append(lax.ppermute(value, 'pairs', route))  12 us
    ppermute x6, starting transfers between devices, along_z(): terms.append(lax.ppermute(value, 'pairs', route))  9.94 us
    pallas_call x1, Pallas kernels, decode(): pl.pallas_call(decode_kernel, grid_spec=pltpu.PrefetchScalarGridSpec(num_...  9.44 us
    ppermute x2, starting transfers between devices, along_y(): return lax.ppermute(value, 'pairs', [(i, i ^ 4) for i in range(8)])  6.37 us
    ppermute x2, waiting for transfers between devices, along_y(): return lax.ppermute(value, 'pairs', [(i, i ^ 4) for i in range(8)])  4.87 us
  transfers between devices with their start and end apart: 37, of which 26 were waited for; matrix products, arithmetic and copies ran while one was open for 0% of the time, Pallas kernels for 4%

profile of v1, /device:TPU:0, one launch (start us, length us, event | category | flops | bytes accessed | tf_op | source)
XLA Modules:
  0.0 151.0 jit_solution(12229607470096260618)
XLA Ops:
  1.5 1.7 %copy-done = f32[512,3,384]{2,0,1:T(8,128)S(1)} copy-done((f32[512,3,384]{2,0,1:T(8,128)S(1)}, f32[512,3,384]{2,0,1:T(8,128)}, u32[]{:S(2)}) %copy-start) | copy-done | bytes 2359320
  3.1 1.2 copy-done.2
  4.4 0.8 copy-done.3
  5.1 0.7 copy-done.5
  5.8 26.5 %contacts.1 = (bf16[512,8192]{1,0:T(8,128)(2,1)S(1)}, f32[64,512]{1,0:T(8,128)S(1)}) custom-call(s32[64]{0:T(128)S(1)} %copy-done.5, s32[1,8192]{1,0:T(1,128)S(1)} %bitcast.124, f32[3,512,384]{2,1,0:T(8,128)S(1)} %bitcast.109, bf16[64,8192]{1,0:T(8,128)(2,1)S(1)} %copy-done.2), custom_call_target="tpu_custom_call" | custom-call | tf_op jit(solution)/shard_map/contacts/pallas_call | solution.py:77
  32.3 3.4 %collective-permute-start = (f32[64,512]{1,0:T(8,128)S(1)}, f32[64,512]{1,0:T(8,128)S(1)}, u32[]{:S(2)}, u32[]{:S(2)}) collective-permute-start(f32[64,512]{1,0:T(8,128)S(1)} %get-tuple-element.19.a_ref), channel_id=1, source_target_pairs={{0,4},{1,5},{2,6},{3,7},{4,0},{5,1},{6,2},{7,3},{8,12},{9,13},{10,... | collective-permute-start | bytes 393224 | tf_op jit(solution)/shard_map/ppermute | solution.py:379
  35.7 3.5 %collective-permute-done.b_ref = f32[64,512]{1,0:T(8,128)S(1)} collective-permute-done((f32[64,512]{1,0:T(8,128)S(1)}, f32[64,512]{1,0:T(8,128)S(1)}, u32[]{:S(2)}, u32[]{:S(2)}) %collective-permute-start) | collective-permute-done | bytes 131104 | tf_op jit(solution)/shard_map/ppermute | solution.py:379
  39.2 4.0 %collective-permute-start.3 = (f32[64,512]{1,0:T(8,128)S(1)}, f32[64,512]{1,0:T(8,128)S(1)}, u32[]{:S(2)}, u32[]{:S(2)}) collective-permute-start(f32[64,512]{1,0:T(8,128)S(1)} %shard_map.95.a_ref), channel_id=1, source_target_pairs={{0,2},{1,3},{2,0},{3,1},{4,6},{5,7},{6,4},{7,5},{8,10},{9,11},{10,... | collective-permute-start | bytes 393224 | tf_op jit(solution)/shard_map/ppermute | solution.py:386
  43.2 0.7 collective-permute-start.2
  43.9 1.3 collective-permute-start.1
  45.2 1.5 %collective-permute-done.3.d_ref = f32[64,512]{1,0:T(8,128)S(1)} collective-permute-done((f32[64,512]{1,0:T(8,128)S(1)}, f32[64,512]{1,0:T(8,128)S(1)}, u32[]{:S(2)}, u32[]{:S(2)}) %collective-permute-start.3) | collective-permute-done | bytes 131104 | tf_op jit(solution)/shard_map/ppermute | solution.py:386
  46.7 2.7 %collective-permute-done.2.c_ref = f32[64,512]{1,0:T(8,128)S(1)} collective-permute-done((f32[64,512]{1,0:T(8,128)S(1)}, f32[64,512]{1,0:T(8,128)S(1)}, u32[]{:S(2)}, u32[]{:S(2)}) %collective-permute-start.2) | collective-permute-done | bytes 131104 | tf_op jit(solution)/shard_map/ppermute | solution.py:386
  49.4 0.7 collective-permute-done.1.b_ref
  50.2 1.3 collective-permute-start.4
  51.5 0.9 collective-permute-done.4.before_ref
  52.4 9.4 %decode.1 = (f32[8,8,4096]{2,1,0:T(8,128)S(1)}, f32[8,8,4096]{2,1,0:T(8,128)S(1)}, f32[64,512]{1,0:T(8,128)S(1)}) custom-call(s32[4]{0:T(128)S(1)} %pad_add_fusion.info_ref, f32[1]{0:T(128)S(6)} %sqrt.3.scale_ref, bf16[64,512]{1,0:T(8,128)(2,1)S(1)} %get-tuple-element.21.latent_ref, bf16[64,512]{1,0:T(8,128)(2,1)S(1)} %collective-permute-done.4.before_ref, ...), custom_call_target="tpu_custom_call" | custom-call | tf_op jit(solution)/shard_map/decode/pallas_call | solution.py:172
  61.8 2.8 %collective-permute-start.12 = (f32[8,8,4096]{2,1,0:T(8,128)S(1)}, f32[8,8,4096]{2,1,0:T(8,128)S(1)}, u32[]{:S(2)}, u32[]{:S(2)}) collective-permute-start(f32[8,8,4096]{2,1,0:T(8,128)S(1)} %get-tuple-element.27), channel_id=1, source_target_pairs={{0,8},{8,0},{16,24},{24,16},{32,40},{40,32},{48,56},{56,48},{64,72... | collective-permute-start | bytes 3145736 | tf_op jit(solution)/shard_map/ppermute | solution.py:298
  64.7 1.3 collective-permute-start.7
  66.0 1.3 collective-permute-start.6
  67.3 3.0 %collective-permute-start.5 = (f32[64,512]{1,0:T(8,128)S(1)}, f32[64,512]{1,0:T(8,128)S(1)}, u32[]{:S(2)}, u32[]{:S(2)}) collective-permute-start(f32[64,512]{1,0:T(8,128)S(1)} %get-tuple-element.23.a_ref), channel_id=1, source_target_pairs={{0,4},{1,5},{2,6},{3,7},{4,0},{5,1},{6,2},{7,3},{8,12},{9,13},{10,... | collective-permute-start | bytes 393224 | tf_op jit(solution)/shard_map/ppermute | solution.py:379
  70.2 2.3 %collective-permute-done.7.d_ref = f32[64,512]{1,0:T(8,128)S(1)} collective-permute-done((f32[64,512]{1,0:T(8,128)S(1)}, f32[64,512]{1,0:T(8,128)S(1)}, u32[]{:S(2)}, u32[]{:S(2)}) %collective-permute-start.7) | collective-permute-done | bytes 131104 | tf_op jit(solution)/shard_map/ppermute | solution.py:392
  72.6 1.4 collective-permute-done.5.b_ref
  74.0 1.9 %collective-permute-start.10 = (f32[64,512]{1,0:T(8,128)S(1)}, f32[64,512]{1,0:T(8,128)S(1)}, u32[]{:S(2)}, u32[]{:S(2)}) collective-permute-start(f32[64,512]{1,0:T(8,128)S(1)} %shard_map.97.a_ref), channel_id=1, source_target_pairs={{0,2},{1,3},{2,0},{3,1},{4,6},{5,7},{6,4},{7,5},{8,10},{9,11},{10,... | collective-permute-start | bytes 393224 | tf_op jit(solution)/shard_map/ppermute | solution.py:386
  75.9 1.2 collective-permute-start.9
  77.2 0.8 collective-permute-start.8
  78.0 2.6 %collective-permute-done.10.d_ref = f32[64,512]{1,0:T(8,128)S(1)} collective-permute-done((f32[64,512]{1,0:T(8,128)S(1)}, f32[64,512]{1,0:T(8,128)S(1)}, u32[]{:S(2)}, u32[]{:S(2)}) %collective-permute-start.10) | collective-permute-done | bytes 131104 | tf_op jit(solution)/shard_map/ppermute | solution.py:386
  80.6 1.4 collective-permute-done.9.c_ref
  82.0 3.0 %collective-permute-done.8.b_ref = f32[64,512]{1,0:T(8,128)S(1)} collective-permute-done((f32[64,512]{1,0:T(8,128)S(1)}, f32[64,512]{1,0:T(8,128)S(1)}, u32[]{:S(2)}, u32[]{:S(2)}) %collective-permute-start.8) | collective-permute-done | bytes 131104 | tf_op jit(solution)/shard_map/ppermute | solution.py:386
  85.1 2.0 %encode_other_half.1 = f32[8,8,4096]{2,1,0:T(8,128)S(1)} custom-call(s32[4]{0:T(128)S(1)} %pad_add_fusion.info_ref, bf16[64,512]{1,0:T(8,128)(2,1)S(1)} %shard_map.98.hidden_ref, bf16[512,8192]{1,0:T(8,128)(2,1)S(1)} %get-tuple-element.22.contact_ref), custom_call_target="tpu_custom_call" | custom-call | tf_op jit(solution)/shard_map/encode_other_half/pallas_call | solution.py:216
  87.1 0.6 collective-permute-start.11
  87.7 2.0 %encode_own_half.1 = f32[8,8,4096]{2,1,0:T(8,128)S(1)} custom-call(s32[4]{0:T(128)S(1)} %pad_add_fusion.info_ref, bf16[64,512]{1,0:T(8,128)(2,1)S(1)} %shard_map.98.hidden_ref, bf16[512,8192]{1,0:T(8,128)(2,1)S(1)} %get-tuple-element.22.contact_ref), custom_call_target="tpu_custom_call" | custom-call | tf_op jit(solution)/shard_map/encode_own_half/pallas_call | solution.py:216
  89.8 0.2 collective-permute-done.11
  90.2 7.8 %collective-permute-start.25 = (f32[2,2,2,8,1280]{4,3,2,1,0:T(8,128)S(1)}, f32[2,2,2,8,1280]{4,3,2,1,0:T(8,128)S(1)}, u32[]{:S(2)}, u32[]{:S(2)}) collective-permute-start(f32[2,2,2,8,1280]{4,3,2,1,0:T(8,128)S(1)} %fusion.15), channel_id=1, source_target_pairs={{0,96},{8,104},{16,112},{24,120},{32,64},{40,72},{48,80},{56,88},{... | collective-permute-start | bytes 983048 | tf_op jit(solution)/shard_map/ppermute | solution.py:294
  98.1 0.8 collective-permute-start.13
  99.0 0.7 collective-permute-start.19
  99.7 6.3 %collective-permute-done.25 = f32[2,2,2,8,1280]{4,3,2,1,0:T(8,128)S(1)} collective-permute-done((f32[2,2,2,8,1280]{4,3,2,1,0:T(8,128)S(1)}, f32[2,2,2,8,1280]{4,3,2,1,0:T(8,128)S(1)}, u32[]{:S(2)}, u32[]{:S(2)}) %collective-permute-start.25) | collective-permute-done | bytes 327712 | tf_op jit(solution)/shard_map/ppermute | solution.py:294
  106.1 0.8 collective-permute-start.26
  106.9 1.4 collective-permute-done.13
  108.4 1.5 collective-permute-start.14
  110.0 1.2 collective-permute-start.20
  111.1 0.7 collective-permute-done.26
  111.9 1.5 collective-permute-start.27
  113.3 1.3 collective-permute-done.14
  114.7 1.0 collective-permute-start.15
  115.7 2.0 %collective-permute-done.20 = f32[2,2,8,1408]{3,2,1,0:T(8,128)S(1)} collective-permute-done((f32[2,2,8,1408]{3,2,1,0:T(8,128)S(1)}, f32[2,2,8,1408]{3,2,1,0:T(8,128)S(1)}, u32[]{:S(2)}, u32[]{:S(2)}) %collective-permute-start.20) | collective-permute-done | bytes 180256 | tf_op jit(solution)/shard_map/ppermute | solution.py:294
  117.9 2.6 %collective-permute-done.15 = f32[2,8,1408]{2,1,0:T(8,128)S(1)} collective-permute-done((f32[2,8,1408]{2,1,0:T(8,128)S(1)}, f32[2,8,1408]{2,1,0:T(8,128)S(1)}, u32[]{:S(2)}, u32[]{:S(2)}) %collective-permute-start.15) | collective-permute-done | bytes 90144 | tf_op jit(solution)/shard_map/ppermute | solution.py:294
  120.5 1.0 collective-permute-start.16
  121.5 1.7 %collective-permute-done.21 = f32[2,8,1408]{2,1,0:T(8,128)S(1)} collective-permute-done((f32[2,8,1408]{2,1,0:T(8,128)S(1)}, f32[2,8,1408]{2,1,0:T(8,128)S(1)}, u32[]{:S(2)}, u32[]{:S(2)}) %collective-permute-start.21) | collective-permute-done | bytes 90144 | tf_op jit(solution)/shard_map/ppermute | solution.py:294
  123.4 2.1 %collective-permute-start.29 = (f32[2,2,8,1280]{3,2,1,0:T(8,128)S(1)}, f32[2,2,8,1280]{3,2,1,0:T(8,128)S(1)}, u32[]{:S(2)}, u32[]{:S(2)}) collective-permute-start(f32[2,2,8,1280]{3,2,1,0:T(8,128)S(1)} %get-tuple-element.41), channel_id=1, source_target_pairs={{0,16},{8,24},{16,0},{24,8},{32,48},{40,56},{48,32},{56,40},{64,80... | collective-permute-start | bytes 491528 | tf_op jit(solution)/shard_map/ppermute | solution.py:294
  125.5 0.9 collective-permute-done.16
  126.4 0.2 collective-permute-start.17
  126.6 1.3 collective-permute-done.22
  127.9 0.7 collective-permute-start.23
  128.6 4.0 %collective-permute-done.17 = f32[2,2,8,1408]{3,2,1,0:T(8,128)S(1)} collective-permute-done((f32[2,2,8,1408]{3,2,1,0:T(8,128)S(1)}, f32[2,2,8,1408]{3,2,1,0:T(8,128)S(1)}, u32[]{:S(2)}, u32[]{:S(2)}) %collective-permute-start.17) | collective-permute-done | bytes 180256 | tf_op jit(solution)/shard_map/ppermute | solution.py:294
  132.6 1.5 collective-permute-start.31
  134.1 0.6 collective-permute-done.23
  134.9 1.3 collective-permute-start.35
  136.4 0.1 collective-permute-done.30.refs_5_
  136.5 0.2 collective-permute-start.24
  136.8 3.3 %collective-permute-done.31 = f32[2,2,2,8,1408]{4,3,2,1,0:T(8,128)S(1)} collective-permute-done((f32[2,2,2,8,1408]{4,3,2,1,0:T(8,128)S(1)}, f32[2,2,2,8,1408]{4,3,2,1,0:T(8,128)S(1)}, u32[]{:S(2)}, u32[]{:S(2)}) %collective-permute-start.31) | collective-permute-done | bytes 360480 | tf_op jit(solution)/shard_map/ppermute | solution.py:294
  140.1 2.1 %collective-permute-done.33 = f32[2,2,2,8,1408]{4,3,2,1,0:T(8,128)S(1)} collective-permute-done((f32[2,2,2,8,1408]{4,3,2,1,0:T(8,128)S(1)}, f32[2,2,2,8,1408]{4,3,2,1,0:T(8,128)S(1)}, u32[]{:S(2)}, u32[]{:S(2)}) %collective-permute-start.33) | collective-permute-done | bytes 360480 | tf_op jit(solution)/shard_map/ppermute | solution.py:294
  142.2 4.0 %collective-permute-done.35 = f32[2,2,2,8,1280]{4,3,2,1,0:T(8,128)S(1)} collective-permute-done((f32[2,2,2,8,1280]{4,3,2,1,0:T(8,128)S(1)}, f32[2,2,2,8,1280]{4,3,2,1,0:T(8,128)S(1)}, u32[]{:S(2)}, u32[]{:S(2)}) %collective-permute-start.35) | collective-permute-done | bytes 327712 | tf_op jit(solution)/shard_map/ppermute | solution.py:294
  146.3 2.3 %assemble.1 = (f32[64,8192]{1,0:T(8,128)}, f32[64,8192]{1,0:T(8,128)}) custom-call(s32[4]{0:T(128)S(1)} %pad_add_fusion.info_ref, f32[4,2,8,1408]{3,2,1,0:T(8,128)S(1)} %bitcast.111, f32[4,2,8,1408]{3,2,1,0:T(8,128)S(1)} %collective-permute-done.18.refs_1_, f32[4,2,8,1408]{3,2,1,0:T(8,128)S(1)} %bitcast.113, ...), custom_call_target="tpu_custom_call" | custom-call | tf_op jit(solution)/shard_map/assemble/pallas_call | solution.py:264
  148.6 2.3 %assemble_rest.1 = (f32[64,8192]{1,0:T(8,128)}, f32[64,8192]{1,0:T(8,128)}) custom-call(s32[4]{0:T(128)S(1)} %pad_add_fusion.info_ref, f32[64,8192]{1,0:T(8,128)} %get-tuple-element.28.refs_0_, f32[64,8192]{1,0:T(8,128)} %get-tuple-element.29.refs_1_, f32[4,2,8,1408]{3,2,1,0:T(8,128)S(1)} %bitcast.119, ...), custom_call_target="tpu_custom_call", output_to_operand_aliasing={{0}: (1, {}), {1}: (2, {})} | custom-call | tf_op jit(solution)/shard_map/assemble_rest/pallas_call | solution.py:264
  (63 shorter events, 1.9 us)
Async XLA Ops:
  0.6 49.5 %copy-start.6 = (f32[64]{0:T(128)S(1)}, f32[64]{0:T(128)}, u32[]{:S(2)}) copy-start(f32[64]{0:T(128)} %param.12) | copy-start | bytes 772
  1.5 1.7 %copy-start = (f32[512,3,384]{2,0,1:T(8,128)S(1)}, f32[512,3,384]{2,0,1:T(8,128)}, u32[]{:S(2)}) copy-start(f32[512,3,384]{2,0,1:T(8,128)} %param.8) | copy-start | bytes 7077892
  3.1 1.2 copy-start.2
  4.4 0.8 copy-start.3
  5.1 0.7 copy-start.5
  5.8 46.6 %copy-start.1 = (bf16[64,8192]{1,0:T(8,128)(2,1)S(1)}, bf16[64,8192]{1,0:T(8,128)(2,1)}, u32[]{:S(2)}) copy-start(bf16[64,8192]{1,0:T(8,128)(2,1)} %dec_ref.1) | copy-start | bytes 3145732
  5.8 46.6 %copy-start.4 = (f32[8192]{0:T(1024)S(1)}, f32[8192]{0:T(1024)}, u32[]{:S(2)}) copy-start(f32[8192]{0:T(1024)} %param.14) | copy-start | bytes 98308
  32.3 6.9 %collective-permute-start = (f32[64,512]{1,0:T(8,128)S(1)}, f32[64,512]{1,0:T(8,128)S(1)}, u32[]{:S(2)}, u32[]{:S(2)}) collective-permute-start(f32[64,512]{1,0:T(8,128)S(1)} %get-tuple-element.19.a_ref), channel_id=1, source_target_pairs={{0,4},{1,5},{2,6},{3,7},{4,0},{5,1},{6,2},{7,3},{8,12},{9,13},{10,... | collective-permute-start | bytes 393224 | tf_op jit(solution)/shard_map/ppermute | solution.py:379
  39.2 7.6 %collective-permute-start.3 = (f32[64,512]{1,0:T(8,128)S(1)}, f32[64,512]{1,0:T(8,128)S(1)}, u32[]{:S(2)}, u32[]{:S(2)}) collective-permute-start(f32[64,512]{1,0:T(8,128)S(1)} %shard_map.95.a_ref), channel_id=1, source_target_pairs={{0,2},{1,3},{2,0},{3,1},{4,6},{5,7},{6,4},{7,5},{8,10},{9,11},{10,... | collective-permute-start | bytes 393224 | tf_op jit(solution)/shard_map/ppermute | solution.py:386
  43.2 6.2 %collective-permute-start.2 = (f32[64,512]{1,0:T(8,128)S(1)}, f32[64,512]{1,0:T(8,128)S(1)}, u32[]{:S(2)}, u32[]{:S(2)}) collective-permute-start(f32[64,512]{1,0:T(8,128)S(1)} %shard_map.95.a_ref), channel_id=1, source_target_pairs={{0,3},{1,0},{2,1},{3,2},{4,7},{5,4},{6,5},{7,6},{8,11},{9,8},{10,9... | collective-permute-start | bytes 393224 | tf_op jit(solution)/shard_map/ppermute | solution.py:386
  43.9 6.2 %collective-permute-start.1 = (f32[64,512]{1,0:T(8,128)S(1)}, f32[64,512]{1,0:T(8,128)S(1)}, u32[]{:S(2)}, u32[]{:S(2)}) collective-permute-start(f32[64,512]{1,0:T(8,128)S(1)} %shard_map.95.a_ref), channel_id=1, source_target_pairs={{0,1},{1,2},{2,3},{3,0},{4,5},{5,6},{6,7},{7,4},{8,9},{9,10},{10,1... | collective-permute-start | bytes 393224 | tf_op jit(solution)/shard_map/ppermute | solution.py:386
  50.2 2.2 %collective-permute-start.4 = (bf16[64,512]{1,0:T(8,128)(2,1)S(1)}, bf16[64,512]{1,0:T(8,128)(2,1)S(1)}, u32[]{:S(2)}, u32[]{:S(2)}) collective-permute-start(bf16[64,512]{1,0:T(8,128)(2,1)S(1)} %get-tuple-element.21.latent_ref), channel_id=1, source_target_pairs={{0,8},{8,16},{16,24},{24,32},{32,40},{40,48},{48,56},{56,64},{64,7... | collective-permute-start | bytes 196616 | tf_op jit(solution)/shard_map/ppermute | solution.py:419
  61.8 27.9 %collective-permute-start.12 = (f32[8,8,4096]{2,1,0:T(8,128)S(1)}, f32[8,8,4096]{2,1,0:T(8,128)S(1)}, u32[]{:S(2)}, u32[]{:S(2)}) collective-permute-start(f32[8,8,4096]{2,1,0:T(8,128)S(1)} %get-tuple-element.27), channel_id=1, source_target_pairs={{0,8},{8,0},{16,24},{24,16},{32,40},{40,32},{48,56},{56,48},{64,72... | collective-permute-start | bytes 3145736 | tf_op jit(solution)/shard_map/ppermute | solution.py:298
  64.7 7.9 %collective-permute-start.7 = (f32[64,512]{1,0:T(8,128)S(1)}, f32[64,512]{1,0:T(8,128)S(1)}, u32[]{:S(2)}, u32[]{:S(2)}) collective-permute-start(f32[64,512]{1,0:T(8,128)S(1)} %get-tuple-element.23.a_ref), channel_id=1, source_target_pairs={{12,0},{13,1},{14,2},{15,3},{8,4},{9,5},{10,6},{11,7},{20,8},{21,9... | collective-permute-start | bytes 393224 | tf_op jit(solution)/shard_map/ppermute | solution.py:392
  66.0 6.6 %collective-permute-start.6 = (f32[64,512]{1,0:T(8,128)S(1)}, f32[64,512]{1,0:T(8,128)S(1)}, u32[]{:S(2)}, u32[]{:S(2)}) collective-permute-start(f32[64,512]{1,0:T(8,128)S(1)} %get-tuple-element.23.a_ref), channel_id=1, source_target_pairs={{8,0},{9,1},{10,2},{11,3},{12,4},{13,5},{14,6},{15,7},{16,8},{17,9... | collective-permute-start | bytes 393224 | tf_op jit(solution)/shard_map/ppermute | solution.py:392
  67.3 6.7 %collective-permute-start.5 = (f32[64,512]{1,0:T(8,128)S(1)}, f32[64,512]{1,0:T(8,128)S(1)}, u32[]{:S(2)}, u32[]{:S(2)}) collective-permute-start(f32[64,512]{1,0:T(8,128)S(1)} %get-tuple-element.23.a_ref), channel_id=1, source_target_pairs={{0,4},{1,5},{2,6},{3,7},{4,0},{5,1},{6,2},{7,3},{8,12},{9,13},{10,... | collective-permute-start | bytes 393224 | tf_op jit(solution)/shard_map/ppermute | solution.py:379
  74.0 6.6 %collective-permute-start.10 = (f32[64,512]{1,0:T(8,128)S(1)}, f32[64,512]{1,0:T(8,128)S(1)}, u32[]{:S(2)}, u32[]{:S(2)}) collective-permute-start(f32[64,512]{1,0:T(8,128)S(1)} %shard_map.97.a_ref), channel_id=1, source_target_pairs={{0,2},{1,3},{2,0},{3,1},{4,6},{5,7},{6,4},{7,5},{8,10},{9,11},{10,... | collective-permute-start | bytes 393224 | tf_op jit(solution)/shard_map/ppermute | solution.py:386
  75.9 6.1 %collective-permute-start.9 = (f32[64,512]{1,0:T(8,128)S(1)}, f32[64,512]{1,0:T(8,128)S(1)}, u32[]{:S(2)}, u32[]{:S(2)}) collective-permute-start(f32[64,512]{1,0:T(8,128)S(1)} %shard_map.97.a_ref), channel_id=1, source_target_pairs={{0,3},{1,0},{2,1},{3,2},{4,7},{5,4},{6,5},{7,6},{8,11},{9,8},{10,9... | collective-permute-start | bytes 393224 | tf_op jit(solution)/shard_map/ppermute | solution.py:386
  77.2 7.9 %collective-permute-start.8 = (f32[64,512]{1,0:T(8,128)S(1)}, f32[64,512]{1,0:T(8,128)S(1)}, u32[]{:S(2)}, u32[]{:S(2)}) collective-permute-start(f32[64,512]{1,0:T(8,128)S(1)} %shard_map.97.a_ref), channel_id=1, source_target_pairs={{0,1},{1,2},{2,3},{3,0},{4,5},{5,6},{6,7},{7,4},{8,9},{9,10},{10,1... | collective-permute-start | bytes 393224 | tf_op jit(solution)/shard_map/ppermute | solution.py:386
  87.1 2.9 %collective-permute-start.11 = (f32[8,8,4096]{2,1,0:T(8,128)S(1)}, f32[8,8,4096]{2,1,0:T(8,128)S(1)}, u32[]{:S(2)}, u32[]{:S(2)}) collective-permute-start(f32[8,8,4096]{2,1,0:T(8,128)S(1)} %encode_other_half.1), channel_id=1, source_target_pairs={{0,8},{8,0},{16,24},{24,16},{32,40},{40,32},{48,56},{56,48},{64,72... | collective-permute-start | bytes 3145736 | tf_op jit(solution)/shard_map/ppermute | solution.py:298
  90.2 15.8 %collective-permute-start.25 = (f32[2,2,2,8,1280]{4,3,2,1,0:T(8,128)S(1)}, f32[2,2,2,8,1280]{4,3,2,1,0:T(8,128)S(1)}, u32[]{:S(2)}, u32[]{:S(2)}) collective-permute-start(f32[2,2,2,8,1280]{4,3,2,1,0:T(8,128)S(1)} %fusion.15), channel_id=1, source_target_pairs={{0,96},{8,104},{16,112},{24,120},{32,64},{40,72},{48,80},{56,88},{... | collective-permute-start | bytes 983048 | tf_op jit(solution)/shard_map/ppermute | solution.py:294
  98.1 10.2 %collective-permute-start.13 = (f32[2,2,2,8,1408]{4,3,2,1,0:T(8,128)S(1)}, f32[2,2,2,8,1408]{4,3,2,1,0:T(8,128)S(1)}, u32[]{:S(2)}, u32[]{:S(2)}) collective-permute-start(f32[2,2,2,8,1408]{4,3,2,1,0:T(8,128)S(1)} %fusion.7), channel_id=1, source_target_pairs={{0,16},{8,24},{16,0},{24,8},{32,48},{40,56},{48,32},{56,40},{64,80... | collective-permute-start | bytes 1081352 | tf_op jit(solution)/shard_map/ppermute | solution.py:294
  99.0 10.9 %collective-permute-start.19 = (f32[2,2,2,8,1408]{4,3,2,1,0:T(8,128)S(1)}, f32[2,2,2,8,1408]{4,3,2,1,0:T(8,128)S(1)}, u32[]{:S(2)}, u32[]{:S(2)}) collective-permute-start(f32[2,2,2,8,1408]{4,3,2,1,0:T(8,128)S(1)} %fusion.6), channel_id=1, source_target_pairs={{0,32},{8,40},{16,48},{24,56},{32,0},{40,8},{48,16},{56,24},{64,96... | collective-permute-start | bytes 1081352 | tf_op jit(solution)/shard_map/ppermute | solution.py:294
  106.1 5.7 %collective-permute-start.26 = (f32[2,2,8,1280]{3,2,1,0:T(8,128)S(1)}, f32[2,2,8,1280]{3,2,1,0:T(8,128)S(1)}, u32[]{:S(2)}, u32[]{:S(2)}) collective-permute-start(f32[2,2,8,1280]{3,2,1,0:T(8,128)S(1)} %slice_bitcast_fusion.4), channel_id=1, source_target_pairs={{0,16},{8,24},{16,0},{24,8},{32,48},{40,56},{48,32},{56,40},{64,80... | collective-permute-start | bytes 491528 | tf_op jit(solution)/shard_map/ppermute | solution.py:294
  108.4 6.3 %collective-permute-start.14 = (f32[2,2,8,1408]{3,2,1,0:T(8,128)S(1)}, f32[2,2,8,1408]{3,2,1,0:T(8,128)S(1)}, u32[]{:S(2)}, u32[]{:S(2)}) collective-permute-start(f32[2,2,8,1408]{3,2,1,0:T(8,128)S(1)} %slice_bitcast_fusion.2), channel_id=1, source_target_pairs={{0,32},{8,40},{16,48},{24,56},{32,0},{40,8},{48,16},{56,24},{64,96... | collective-permute-start | bytes 540680 | tf_op jit(solution)/shard_map/ppermute | solution.py:294
  110.0 7.7 %collective-permute-start.20 = (f32[2,2,8,1408]{3,2,1,0:T(8,128)S(1)}, f32[2,2,8,1408]{3,2,1,0:T(8,128)S(1)}, u32[]{:S(2)}, u32[]{:S(2)}) collective-permute-start(f32[2,2,8,1408]{3,2,1,0:T(8,128)S(1)} %slice_bitcast_fusion), channel_id=1, source_target_pairs={{0,96},{8,104},{16,112},{24,120},{32,64},{40,72},{48,80},{56,88},{... | collective-permute-start | bytes 540680 | tf_op jit(solution)/shard_map/ppermute | solution.py:294
  111.9 5.9 %collective-permute-start.27 = (f32[2,8,1280]{2,1,0:T(8,128)S(1)}, f32[2,8,1280]{2,1,0:T(8,128)S(1)}, u32[]{:S(2)}, u32[]{:S(2)}) collective-permute-start(f32[2,8,1280]{2,1,0:T(8,128)S(1)} %slice_bitcast_fusion.10), channel_id=1, source_target_pairs={{0,32},{8,40},{16,48},{24,56},{32,0},{40,8},{48,16},{56,24},{64,96... | collective-permute-start | bytes 245768 | tf_op jit(solution)/shard_map/ppermute | solution.py:294
  114.7 5.8 %collective-permute-start.15 = (f32[2,8,1408]{2,1,0:T(8,128)S(1)}, f32[2,8,1408]{2,1,0:T(8,128)S(1)}, u32[]{:S(2)}, u32[]{:S(2)}) collective-permute-start(f32[2,8,1408]{2,1,0:T(8,128)S(1)} %slice_bitcast_fusion.8), channel_id=1, source_target_pairs={{0,96},{8,104},{16,112},{24,120},{32,64},{40,72},{48,80},{56,88},{... | collective-permute-start | bytes 270344 | tf_op jit(solution)/shard_map/ppermute | solution.py:294
  117.7 5.6 %collective-permute-start.21 = (f32[2,8,1408]{2,1,0:T(8,128)S(1)}, f32[2,8,1408]{2,1,0:T(8,128)S(1)}, u32[]{:S(2)}, u32[]{:S(2)}) collective-permute-start(f32[2,8,1408]{2,1,0:T(8,128)S(1)} %slice_bitcast_fusion.6), channel_id=1, source_target_pairs={{0,16},{8,24},{16,0},{24,8},{32,48},{40,56},{48,32},{56,40},{64,80... | collective-permute-start | bytes 270344 | tf_op jit(solution)/shard_map/ppermute | solution.py:294
  117.8 5.6 %collective-permute-start.28 = (f32[2,8,1280]{2,1,0:T(8,128)S(1)}, f32[2,8,1280]{2,1,0:T(8,128)S(1)}, u32[]{:S(2)}, u32[]{:S(2)}) collective-permute-start(f32[2,8,1280]{2,1,0:T(8,128)S(1)} %fusion.23), channel_id=1, source_target_pairs={{0,32},{8,40},{16,48},{24,56},{32,0},{40,8},{48,16},{56,24},{64,96... | collective-permute-start | bytes 245768 | tf_op jit(solution)/shard_map/ppermute | solution.py:294
  120.5 5.8 %collective-permute-start.16 = (f32[2,8,1408]{2,1,0:T(8,128)S(1)}, f32[2,8,1408]{2,1,0:T(8,128)S(1)}, u32[]{:S(2)}, u32[]{:S(2)}) collective-permute-start(f32[2,8,1408]{2,1,0:T(8,128)S(1)} %fusion.22), channel_id=1, source_target_pairs={{0,96},{8,104},{16,112},{24,120},{32,64},{40,72},{48,80},{56,88},{... | collective-permute-start | bytes 270344 | tf_op jit(solution)/shard_map/ppermute | solution.py:294
  123.2 4.6 %collective-permute-start.22 = (f32[2,8,1408]{2,1,0:T(8,128)S(1)}, f32[2,8,1408]{2,1,0:T(8,128)S(1)}, u32[]{:S(2)}, u32[]{:S(2)}) collective-permute-start(f32[2,8,1408]{2,1,0:T(8,128)S(1)} %fusion.21), channel_id=1, source_target_pairs={{0,16},{8,24},{16,0},{24,8},{32,48},{40,56},{48,32},{56,40},{64,80... | collective-permute-start | bytes 270344 | tf_op jit(solution)/shard_map/ppermute | solution.py:294
  123.4 11.4 %collective-permute-start.29 = (f32[2,2,8,1280]{3,2,1,0:T(8,128)S(1)}, f32[2,2,8,1280]{3,2,1,0:T(8,128)S(1)}, u32[]{:S(2)}, u32[]{:S(2)}) collective-permute-start(f32[2,2,8,1280]{3,2,1,0:T(8,128)S(1)} %get-tuple-element.41), channel_id=1, source_target_pairs={{0,16},{8,24},{16,0},{24,8},{32,48},{40,56},{48,32},{56,40},{64,80... | collective-permute-start | bytes 491528 | tf_op jit(solution)/shard_map/ppermute | solution.py:294
  126.4 6.2 %collective-permute-start.17 = (f32[2,2,8,1408]{3,2,1,0:T(8,128)S(1)}, f32[2,2,8,1408]{3,2,1,0:T(8,128)S(1)}, u32[]{:S(2)}, u32[]{:S(2)}) collective-permute-start(f32[2,2,8,1408]{3,2,1,0:T(8,128)S(1)} %get-tuple-element.39), channel_id=1, source_target_pairs={{0,32},{8,40},{16,48},{24,56},{32,0},{40,8},{48,16},{56,24},{64,96... | collective-permute-start | bytes 540680 | tf_op jit(solution)/shard_map/ppermute | solution.py:294
  127.9 6.8 %collective-permute-start.23 = (f32[2,2,8,1408]{3,2,1,0:T(8,128)S(1)}, f32[2,2,8,1408]{3,2,1,0:T(8,128)S(1)}, u32[]{:S(2)}, u32[]{:S(2)}) collective-permute-start(f32[2,2,8,1408]{3,2,1,0:T(8,128)S(1)} %get-tuple-element.37), channel_id=1, source_target_pairs={{0,96},{8,104},{16,112},{24,120},{32,64},{40,72},{48,80},{56,88},{... | collective-permute-start | bytes 540680 | tf_op jit(solution)/shard_map/ppermute | solution.py:294
  132.6 7.5 %collective-permute-start.31 = (f32[2,2,2,8,1408]{4,3,2,1,0:T(8,128)S(1)}, f32[2,2,2,8,1408]{4,3,2,1,0:T(8,128)S(1)}, u32[]{:S(2)}, u32[]{:S(2)}) collective-permute-start(f32[2,2,2,8,1408]{4,3,2,1,0:T(8,128)S(1)} %pad_maximum_fusion.2), channel_id=1, source_target_pairs={{0,16},{8,24},{16,0},{24,8},{32,48},{40,56},{48,32},{56,40},{64,80... | collective-permute-start | bytes 1081352 | tf_op jit(solution)/shard_map/ppermute | solution.py:294
  134.7 7.5 %collective-permute-start.33 = (f32[2,2,2,8,1408]{4,3,2,1,0:T(8,128)S(1)}, f32[2,2,2,8,1408]{4,3,2,1,0:T(8,128)S(1)}, u32[]{:S(2)}, u32[]{:S(2)}) collective-permute-start(f32[2,2,2,8,1408]{4,3,2,1,0:T(8,128)S(1)} %pad_maximum_fusion.3), channel_id=1, source_target_pairs={{0,32},{8,40},{16,48},{24,56},{32,0},{40,8},{48,16},{56,24},{64,96... | collective-permute-start | bytes 1081352 | tf_op jit(solution)/shard_map/ppermute | solution.py:294
  134.8 1.7 %collective-permute-start.30 = (f32[4,2,8,1280]{3,2,1,0:T(8,128)S(1)}, f32[4,2,8,1280]{3,2,1,0:T(8,128)S(1)}, u32[]{:S(2)}, u32[]{:S(2)}) collective-permute-start(f32[4,2,8,1280]{3,2,1,0:T(8,128)S(1)} %bitcast.114), channel_id=1, source_target_pairs={{0,8},{8,0},{16,24},{24,16},{32,40},{40,32},{48,56},{56,48},{64,72... | collective-permute-start | bytes 983048 | tf_op jit(solution)/shard_map/ppermute | solution.py:298
  134.9 11.3 %collective-permute-start.35 = (f32[2,2,2,8,1280]{4,3,2,1,0:T(8,128)S(1)}, f32[2,2,2,8,1280]{4,3,2,1,0:T(8,128)S(1)}, u32[]{:S(2)}, u32[]{:S(2)}) collective-permute-start(f32[2,2,2,8,1280]{4,3,2,1,0:T(8,128)S(1)} %pad_maximum_fusion.5), channel_id=1, source_target_pairs={{0,96},{8,104},{16,112},{24,120},{32,64},{40,72},{48,80},{56,88},{... | collective-permute-start | bytes 983048 | tf_op jit(solution)/shard_map/ppermute | solution.py:294
  136.3 10.0 %collective-permute-start.18 = (f32[4,2,8,1408]{3,2,1,0:T(8,128)S(1)}, f32[4,2,8,1408]{3,2,1,0:T(8,128)S(1)}, u32[]{:S(2)}, u32[]{:S(2)}) collective-permute-start(f32[4,2,8,1408]{3,2,1,0:T(8,128)S(1)} %bitcast.110), channel_id=1, source_target_pairs={{0,8},{8,0},{16,24},{24,16},{32,40},{40,32},{48,56},{56,48},{64,72... | collective-permute-start | bytes 1081352 | tf_op jit(solution)/shard_map/ppermute | solution.py:298
  136.5 9.7 %collective-permute-start.24 = (f32[4,2,8,1408]{3,2,1,0:T(8,128)S(1)}, f32[4,2,8,1408]{3,2,1,0:T(8,128)S(1)}, u32[]{:S(2)}, u32[]{:S(2)}) collective-permute-start(f32[4,2,8,1408]{3,2,1,0:T(8,128)S(1)} %bitcast.112), channel_id=1, source_target_pairs={{0,8},{8,0},{16,24},{24,16},{32,40},{40,32},{48,56},{56,48},{64,72... | collective-permute-start | bytes 1081352 | tf_op jit(solution)/shard_map/ppermute | solution.py:298
  140.1 8.5 %collective-permute-start.32 = (f32[4,2,8,1408]{3,2,1,0:T(8,128)S(1)}, f32[4,2,8,1408]{3,2,1,0:T(8,128)S(1)}, u32[]{:S(2)}, u32[]{:S(2)}) collective-permute-start(f32[4,2,8,1408]{3,2,1,0:T(8,128)S(1)} %bitcast.118), channel_id=1, source_target_pairs={{0,8},{8,0},{16,24},{24,16},{32,40},{40,32},{48,56},{56,48},{64,72... | collective-permute-start | bytes 1081352 | tf_op jit(solution)/shard_map/ppermute | solution.py:298
  142.2 6.4 %collective-permute-start.34 = (f32[4,2,8,1408]{3,2,1,0:T(8,128)S(1)}, f32[4,2,8,1408]{3,2,1,0:T(8,128)S(1)}, u32[]{:S(2)}, u32[]{:S(2)}) collective-permute-start(f32[4,2,8,1408]{3,2,1,0:T(8,128)S(1)} %bitcast.120), channel_id=1, source_target_pairs={{0,8},{8,0},{16,24},{24,16},{32,40},{40,32},{48,56},{56,48},{64,72... | collective-permute-start | bytes 1081352 | tf_op jit(solution)/shard_map/ppermute | solution.py:298
  146.3 2.3 %collective-permute-start.36 = (f32[4,2,8,1280]{3,2,1,0:T(8,128)S(1)}, f32[4,2,8,1280]{3,2,1,0:T(8,128)S(1)}, u32[]{:S(2)}, u32[]{:S(2)}) collective-permute-start(f32[4,2,8,1280]{3,2,1,0:T(8,128)S(1)} %bitcast.122), channel_id=1, source_target_pairs={{0,8},{8,0},{16,24},{24,16},{32,40},{40,32},{48,56},{56,48},{64,72... | collective-permute-start | bytes 983048 | tf_op jit(solution)/shard_map/ppermute | solution.py:298

commit v2 on v1

--- a/solution.py
+++ b/solution.py
@@ -121,8 +121,9 @@
 
     @pl.when(block == 0)
     def _():
-        own = pltpu.roll(latent_ref[...].astype(F32), lag, 1)
-        before = pltpu.roll(before_ref[...].astype(F32), lag, 1)
+        turn = lax.rem(lag, frames)
+        own = pltpu.roll(latent_ref[...].astype(F32), turn, 1)
+        before = pltpu.roll(before_ref[...].astype(F32), turn, 1)
         frame = lax.broadcasted_iota(jnp.int32, (latents, frames), 1)
         value = jnp.where(frame >= lag, own, before)
         rolled[...] = value.astype(BF)

time: 153 us -> 153 us (level)
  transfers between devices with their start and end apart: 37 -> 37, of which waited for: 26 -> 25; matrix products, arithmetic and copies ran while one was open for 0% -> 0% of each run, Pallas kernels for 4% -> 4%
where the time goes in v2:
time: 153 us; the launch traced here: 151 us
  waiting for transfers between devices  52 us (34%)
  starting transfers between devices  47.1 us (31%)
  Pallas kernels  44.7 us (29%)
  local copies, waits for them, and re-layouts  4.38 us (3%)
  between operations  1.88 us (1%)
    ppermute x18, waiting for transfers between devices, flip(): return lax.ppermute(value, 'frames', route)  31.7 us
    pallas_call x1, Pallas kernels, contacts_and_sum(): pl.pallas_call(contact_kernel, grid_spec=pltpu.PrefetchScalarGridSpec(num...  26.5 us
    ppermute x18, starting transfers between devices, flip(): return lax.ppermute(value, 'frames', route)  22.9 us
    ppermute x6, waiting for transfers between devices, along_z(): terms.append(lax.ppermute(value, 'pairs', route))  12 us
    ppermute x6, starting transfers between devices, along_z(): terms.append(lax.ppermute(value, 'pairs', route))  9.94 us
    pallas_call x1, Pallas kernels, decode(): pl.pallas_call(decode_kernel, grid_spec=pltpu.PrefetchScalarGridSpec(num_...  9.44 us
    ppermute x2, starting transfers between devices, along_y(): return lax.ppermute(value, 'pairs', [(i, i ^ 4) for i in range(8)])  6.37 us
    ppermute x2, waiting for transfers between devices, along_y(): return lax.ppermute(value, 'pairs', [(i, i ^ 4) for i in range(8)])  4.87 us
  transfers between devices with their start and end apart: 37, of which 25 were waited for; matrix products, arithmetic and copies ran while one was open for 0% of the time, Pallas kernels for 4%

profile of v2, /device:TPU:0, one launch (start us, length us, event | category | flops | bytes accessed | tf_op | source)
XLA Modules:
  0.0 150.9 jit_solution(12925249052574465789)
XLA Ops:
  1.5 1.7 %copy-done = f32[512,3,384]{2,0,1:T(8,128)S(1)} copy-done((f32[512,3,384]{2,0,1:T(8,128)S(1)}, f32[512,3,384]{2,0,1:T(8,128)}, u32[]{:S(2)}) %copy-start) | copy-done | bytes 2359320
  3.1 1.2 copy-done.2
  4.4 0.8 copy-done.3
  5.1 0.7 copy-done.5
  5.8 26.5 %contacts.1 = (bf16[512,8192]{1,0:T(8,128)(2,1)S(1)}, f32[64,512]{1,0:T(8,128)S(1)}) custom-call(s32[64]{0:T(128)S(1)} %copy-done.5, s32[1,8192]{1,0:T(1,128)S(1)} %bitcast.124, f32[3,512,384]{2,1,0:T(8,128)S(1)} %bitcast.109, bf16[64,8192]{1,0:T(8,128)(2,1)S(1)} %copy-done.2), custom_call_target="tpu_custom_call" | custom-call | tf_op jit(solution)/shard_map/contacts/pallas_call | solution.py:77
  32.3 3.4 %collective-permute-start = (f32[64,512]{1,0:T(8,128)S(1)}, f32[64,512]{1,0:T(8,128)S(1)}, u32[]{:S(2)}, u32[]{:S(2)}) collective-permute-start(f32[64,512]{1,0:T(8,128)S(1)} %get-tuple-element.19.a_ref), channel_id=1, source_target_pairs={{0,4},{1,5},{2,6},{3,7},{4,0},{5,1},{6,2},{7,3},{8,12},{9,13},{10,... | collective-permute-start | bytes 393224 | tf_op jit(solution)/shard_map/ppermute | solution.py:380
  35.7 3.5 %collective-permute-done.b_ref = f32[64,512]{1,0:T(8,128)S(1)} collective-permute-done((f32[64,512]{1,0:T(8,128)S(1)}, f32[64,512]{1,0:T(8,128)S(1)}, u32[]{:S(2)}, u32[]{:S(2)}) %collective-permute-start) | collective-permute-done | bytes 131104 | tf_op jit(solution)/shard_map/ppermute | solution.py:380
  39.2 4.0 %collective-permute-start.3 = (f32[64,512]{1,0:T(8,128)S(1)}, f32[64,512]{1,0:T(8,128)S(1)}, u32[]{:S(2)}, u32[]{:S(2)}) collective-permute-start(f32[64,512]{1,0:T(8,128)S(1)} %shard_map.95.a_ref), channel_id=1, source_target_pairs={{0,2},{1,3},{2,0},{3,1},{4,6},{5,7},{6,4},{7,5},{8,10},{9,11},{10,... | collective-permute-start | bytes 393224 | tf_op jit(solution)/shard_map/ppermute | solution.py:387
  43.2 0.7 collective-permute-start.2
  43.9 1.3 collective-permute-start.1
  45.2 1.5 %collective-permute-done.3.d_ref = f32[64,512]{1,0:T(8,128)S(1)} collective-permute-done((f32[64,512]{1,0:T(8,128)S(1)}, f32[64,512]{1,0:T(8,128)S(1)}, u32[]{:S(2)}, u32[]{:S(2)}) %collective-permute-start.3) | collective-permute-done | bytes 131104 | tf_op jit(solution)/shard_map/ppermute | solution.py:387
  46.7 2.7 %collective-permute-done.2.c_ref = f32[64,512]{1,0:T(8,128)S(1)} collective-permute-done((f32[64,512]{1,0:T(8,128)S(1)}, f32[64,512]{1,0:T(8,128)S(1)}, u32[]{:S(2)}, u32[]{:S(2)}) %collective-permute-start.2) | collective-permute-done | bytes 131104 | tf_op jit(solution)/shard_map/ppermute | solution.py:387
  49.4 0.7 collective-permute-done.1.b_ref
  50.2 1.3 collective-permute-start.4
  51.5 0.9 collective-permute-done.4.before_ref
  52.4 9.4 %decode.1 = (f32[8,8,4096]{2,1,0:T(8,128)S(1)}, f32[8,8,4096]{2,1,0:T(8,128)S(1)}, f32[64,512]{1,0:T(8,128)S(1)}) custom-call(s32[4]{0:T(128)S(1)} %pad_add_fusion.info_ref, f32[1]{0:T(128)S(6)} %sqrt.3.scale_ref, bf16[64,512]{1,0:T(8,128)(2,1)S(1)} %get-tuple-element.21.latent_ref, bf16[64,512]{1,0:T(8,128)(2,1)S(1)} %collective-permute-done.4.before_ref, ...), custom_call_target="tpu_custom_call" | custom-call | tf_op jit(solution)/shard_map/decode/pallas_call | solution.py:173
  61.8 2.8 %collective-permute-start.12 = (f32[8,8,4096]{2,1,0:T(8,128)S(1)}, f32[8,8,4096]{2,1,0:T(8,128)S(1)}, u32[]{:S(2)}, u32[]{:S(2)}) collective-permute-start(f32[8,8,4096]{2,1,0:T(8,128)S(1)} %get-tuple-element.27), channel_id=1, source_target_pairs={{0,8},{8,0},{16,24},{24,16},{32,40},{40,32},{48,56},{56,48},{64,72... | collective-permute-start | bytes 3145736 | tf_op jit(solution)/shard_map/ppermute | solution.py:299
  64.7 1.3 collective-permute-start.7
  66.0 1.3 collective-permute-start.6
  67.3 3.0 %collective-permute-start.5 = (f32[64,512]{1,0:T(8,128)S(1)}, f32[64,512]{1,0:T(8,128)S(1)}, u32[]{:S(2)}, u32[]{:S(2)}) collective-permute-start(f32[64,512]{1,0:T(8,128)S(1)} %get-tuple-element.23.a_ref), channel_id=1, source_target_pairs={{0,4},{1,5},{2,6},{3,7},{4,0},{5,1},{6,2},{7,3},{8,12},{9,13},{10,... | collective-permute-start | bytes 393224 | tf_op jit(solution)/shard_map/ppermute | solution.py:380
  70.2 2.3 %collective-permute-done.7.d_ref = f32[64,512]{1,0:T(8,128)S(1)} collective-permute-done((f32[64,512]{1,0:T(8,128)S(1)}, f32[64,512]{1,0:T(8,128)S(1)}, u32[]{:S(2)}, u32[]{:S(2)}) %collective-permute-start.7) | collective-permute-done | bytes 131104 | tf_op jit(solution)/shard_map/ppermute | solution.py:393
  72.6 1.4 collective-permute-done.5.b_ref
  74.0 1.9 %collective-permute-start.10 = (f32[64,512]{1,0:T(8,128)S(1)}, f32[64,512]{1,0:T(8,128)S(1)}, u32[]{:S(2)}, u32[]{:S(2)}) collective-permute-start(f32[64,512]{1,0:T(8,128)S(1)} %shard_map.97.a_ref), channel_id=1, source_target_pairs={{0,2},{1,3},{2,0},{3,1},{4,6},{5,7},{6,4},{7,5},{8,10},{9,11},{10,... | collective-permute-start | bytes 393224 | tf_op jit(solution)/shard_map/ppermute | solution.py:387
  75.9 1.2 collective-permute-start.9
  77.2 0.8 collective-permute-start.8
  78.0 2.6 %collective-permute-done.10.d_ref = f32[64,512]{1,0:T(8,128)S(1)} collective-permute-done((f32[64,512]{1,0:T(8,128)S(1)}, f32[64,512]{1,0:T(8,128)S(1)}, u32[]{:S(2)}, u32[]{:S(2)}) %collective-permute-start.10) | collective-permute-done | bytes 131104 | tf_op jit(solution)/shard_map/ppermute | solution.py:387
  80.6 1.4 collective-permute-done.9.c_ref
  82.0 3.1 %collective-permute-done.8.b_ref = f32[64,512]{1,0:T(8,128)S(1)} collective-permute-done((f32[64,512]{1,0:T(8,128)S(1)}, f32[64,512]{1,0:T(8,128)S(1)}, u32[]{:S(2)}, u32[]{:S(2)}) %collective-permute-start.8) | collective-permute-done | bytes 131104 | tf_op jit(solution)/shard_map/ppermute | solution.py:387
  85.1 2.0 %encode_other_half.1 = f32[8,8,4096]{2,1,0:T(8,128)S(1)} custom-call(s32[4]{0:T(128)S(1)} %pad_add_fusion.info_ref, bf16[64,512]{1,0:T(8,128)(2,1)S(1)} %shard_map.98.hidden_ref, bf16[512,8192]{1,0:T(8,128)(2,1)S(1)} %get-tuple-element.22.contact_ref), custom_call_target="tpu_custom_call" | custom-call | tf_op jit(solution)/shard_map/encode_other_half/pallas_call | solution.py:217
  87.1 0.6 collective-permute-start.11
  87.7 2.0 %encode_own_half.1 = f32[8,8,4096]{2,1,0:T(8,128)S(1)} custom-call(s32[4]{0:T(128)S(1)} %pad_add_fusion.info_ref, bf16[64,512]{1,0:T(8,128)(2,1)S(1)} %shard_map.98.hidden_ref, bf16[512,8192]{1,0:T(8,128)(2,1)S(1)} %get-tuple-element.22.contact_ref), custom_call_target="tpu_custom_call" | custom-call | tf_op jit(solution)/shard_map/encode_own_half/pallas_call | solution.py:217
  89.8 0.2 collective-permute-done.11
  90.2 7.8 %collective-permute-start.25 = (f32[2,2,2,8,1280]{4,3,2,1,0:T(8,128)S(1)}, f32[2,2,2,8,1280]{4,3,2,1,0:T(8,128)S(1)}, u32[]{:S(2)}, u32[]{:S(2)}) collective-permute-start(f32[2,2,2,8,1280]{4,3,2,1,0:T(8,128)S(1)} %fusion.15), channel_id=1, source_target_pairs={{0,96},{8,104},{16,112},{24,120},{32,64},{40,72},{48,80},{56,88},{... | collective-permute-start | bytes 983048 | tf_op jit(solution)/shard_map/ppermute | solution.py:295
  98.1 0.8 collective-permute-start.13
  99.0 0.7 collective-permute-start.19
  99.7 6.3 %collective-permute-done.25 = f32[2,2,2,8,1280]{4,3,2,1,0:T(8,128)S(1)} collective-permute-done((f32[2,2,2,8,1280]{4,3,2,1,0:T(8,128)S(1)}, f32[2,2,2,8,1280]{4,3,2,1,0:T(8,128)S(1)}, u32[]{:S(2)}, u32[]{:S(2)}) %collective-permute-start.25) | collective-permute-done | bytes 327712 | tf_op jit(solution)/shard_map/ppermute | solution.py:295
  106.1 0.8 collective-permute-start.26
  106.9 1.4 collective-permute-done.13
  108.4 1.5 collective-permute-start.14
  109.9 1.2 collective-permute-start.20
  111.1 0.7 collective-permute-done.26
  111.9 1.4 collective-permute-start.27
  113.3 1.3 collective-permute-done.14
  114.7 1.0 collective-permute-start.15
  115.7 1.9 %collective-permute-done.20 = f32[2,2,8,1408]{3,2,1,0:T(8,128)S(1)} collective-permute-done((f32[2,2,8,1408]{3,2,1,0:T(8,128)S(1)}, f32[2,2,8,1408]{3,2,1,0:T(8,128)S(1)}, u32[]{:S(2)}, u32[]{:S(2)}) %collective-permute-start.20) | collective-permute-done | bytes 180256 | tf_op jit(solution)/shard_map/ppermute | solution.py:295
  117.7 0.2 collective-permute-start.28
  117.9 2.6 %collective-permute-done.15 = f32[2,8,1408]{2,1,0:T(8,128)S(1)} collective-permute-done((f32[2,8,1408]{2,1,0:T(8,128)S(1)}, f32[2,8,1408]{2,1,0:T(8,128)S(1)}, u32[]{:S(2)}, u32[]{:S(2)}) %collective-permute-start.15) | collective-permute-done | bytes 90144 | tf_op jit(solution)/shard_map/ppermute | solution.py:295
  120.5 1.0 collective-permute-start.16
  121.5 1.7 %collective-permute-done.21 = f32[2,8,1408]{2,1,0:T(8,128)S(1)} collective-permute-done((f32[2,8,1408]{2,1,0:T(8,128)S(1)}, f32[2,8,1408]{2,1,0:T(8,128)S(1)}, u32[]{:S(2)}, u32[]{:S(2)}) %collective-permute-start.21) | collective-permute-done | bytes 90144 | tf_op jit(solution)/shard_map/ppermute | solution.py:295
  123.3 2.1 %collective-permute-start.29 = (f32[2,2,8,1280]{3,2,1,0:T(8,128)S(1)}, f32[2,2,8,1280]{3,2,1,0:T(8,128)S(1)}, u32[]{:S(2)}, u32[]{:S(2)}) collective-permute-start(f32[2,2,8,1280]{3,2,1,0:T(8,128)S(1)} %get-tuple-element.41), channel_id=1, source_target_pairs={{0,16},{8,24},{16,0},{24,8},{32,48},{40,56},{48,32},{56,40},{64,80... | collective-permute-start | bytes 491528 | tf_op jit(solution)/shard_map/ppermute | solution.py:295
  125.4 0.9 collective-permute-done.16
  126.4 0.2 collective-permute-start.17
  126.6 1.2 collective-permute-done.22
  127.8 0.7 collective-permute-start.23
  128.6 3.9 %collective-permute-done.17 = f32[2,2,8,1408]{3,2,1,0:T(8,128)S(1)} collective-permute-done((f32[2,2,8,1408]{3,2,1,0:T(8,128)S(1)}, f32[2,2,8,1408]{3,2,1,0:T(8,128)S(1)}, u32[]{:S(2)}, u32[]{:S(2)}) %collective-permute-start.17) | collective-permute-done | bytes 180256 | tf_op jit(solution)/shard_map/ppermute | solution.py:295
  132.5 1.7 %collective-permute-start.31 = (f32[2,2,2,8,1408]{4,3,2,1,0:T(8,128)S(1)}, f32[2,2,2,8,1408]{4,3,2,1,0:T(8,128)S(1)}, u32[]{:S(2)}, u32[]{:S(2)}) collective-permute-start(f32[2,2,2,8,1408]{4,3,2,1,0:T(8,128)S(1)} %pad_maximum_fusion.2), channel_id=1, source_target_pairs={{0,16},{8,24},{16,0},{24,8},{32,48},{40,56},{48,32},{56,40},{64,80... | collective-permute-start | bytes 1081352 | tf_op jit(solution)/shard_map/ppermute | solution.py:295
  134.2 0.4 collective-permute-done.23
  134.9 1.5 collective-permute-start.35
  136.5 0.4 collective-permute-start.24
  136.9 3.1 %collective-permute-done.31 = f32[2,2,2,8,1408]{4,3,2,1,0:T(8,128)S(1)} collective-permute-done((f32[2,2,2,8,1408]{4,3,2,1,0:T(8,128)S(1)}, f32[2,2,2,8,1408]{4,3,2,1,0:T(8,128)S(1)}, u32[]{:S(2)}, u32[]{:S(2)}) %collective-permute-start.31) | collective-permute-done | bytes 360480 | tf_op jit(solution)/shard_map/ppermute | solution.py:295
  140.0 2.1 %collective-permute-done.33 = f32[2,2,2,8,1408]{4,3,2,1,0:T(8,128)S(1)} collective-permute-done((f32[2,2,2,8,1408]{4,3,2,1,0:T(8,128)S(1)}, f32[2,2,2,8,1408]{4,3,2,1,0:T(8,128)S(1)}, u32[]{:S(2)}, u32[]{:S(2)}) %collective-permute-start.33) | collective-permute-done | bytes 360480 | tf_op jit(solution)/shard_map/ppermute | solution.py:295
  142.2 4.0 %collective-permute-done.35 = f32[2,2,2,8,1280]{4,3,2,1,0:T(8,128)S(1)} collective-permute-done((f32[2,2,2,8,1280]{4,3,2,1,0:T(8,128)S(1)}, f32[2,2,2,8,1280]{4,3,2,1,0:T(8,128)S(1)}, u32[]{:S(2)}, u32[]{:S(2)}) %collective-permute-start.35) | collective-permute-done | bytes 327712 | tf_op jit(solution)/shard_map/ppermute | solution.py:295
  146.2 2.3 %assemble.1 = (f32[64,8192]{1,0:T(8,128)}, f32[64,8192]{1,0:T(8,128)}) custom-call(s32[4]{0:T(128)S(1)} %pad_add_fusion.info_ref, f32[4,2,8,1408]{3,2,1,0:T(8,128)S(1)} %bitcast.111, f32[4,2,8,1408]{3,2,1,0:T(8,128)S(1)} %collective-permute-done.18.refs_1_, f32[4,2,8,1408]{3,2,1,0:T(8,128)S(1)} %bitcast.113, ...), custom_call_target="tpu_custom_call" | custom-call | tf_op jit(solution)/shard_map/assemble/pallas_call | solution.py:265
  148.5 2.3 %assemble_rest.1 = (f32[64,8192]{1,0:T(8,128)}, f32[64,8192]{1,0:T(8,128)}) custom-call(s32[4]{0:T(128)S(1)} %pad_add_fusion.info_ref, f32[64,8192]{1,0:T(8,128)} %get-tuple-element.28.refs_0_, f32[64,8192]{1,0:T(8,128)} %get-tuple-element.29.refs_1_, f32[4,2,8,1408]{3,2,1,0:T(8,128)S(1)} %bitcast.119, ...), custom_call_target="tpu_custom_call", output_to_operand_aliasing={{0}: (1, {}), {1}: (2, {})} | custom-call | tf_op jit(solution)/shard_map/assemble_rest/pallas_call | solution.py:265
  (63 shorter events, 1.8 us)
Async XLA Ops:
  0.6 49.5 %copy-start.6 = (f32[64]{0:T(128)S(1)}, f32[64]{0:T(128)}, u32[]{:S(2)}) copy-start(f32[64]{0:T(128)} %param.12) | copy-start | bytes 772
  1.5 1.7 %copy-start = (f32[512,3,384]{2,0,1:T(8,128)S(1)}, f32[512,3,384]{2,0,1:T(8,128)}, u32[]{:S(2)}) copy-start(f32[512,3,384]{2,0,1:T(8,128)} %param.8) | copy-start | bytes 7077892
  3.1 1.2 copy-start.2
  4.4 0.8 copy-start.3
  5.1 0.7 copy-start.5
  5.8 46.6 %copy-start.1 = (bf16[64,8192]{1,0:T(8,128)(2,1)S(1)}, bf16[64,8192]{1,0:T(8,128)(2,1)}, u32[]{:S(2)}) copy-start(bf16[64,8192]{1,0:T(8,128)(2,1)} %dec_ref.1) | copy-start | bytes 3145732
  5.8 46.6 %copy-start.4 = (f32[8192]{0:T(1024)S(1)}, f32[8192]{0:T(1024)}, u32[]{:S(2)}) copy-start(f32[8192]{0:T(1024)} %param.14) | copy-start | bytes 98308
  32.3 6.9 %collective-permute-start = (f32[64,512]{1,0:T(8,128)S(1)}, f32[64,512]{1,0:T(8,128)S(1)}, u32[]{:S(2)}, u32[]{:S(2)}) collective-permute-start(f32[64,512]{1,0:T(8,128)S(1)} %get-tuple-element.19.a_ref), channel_id=1, source_target_pairs={{0,4},{1,5},{2,6},{3,7},{4,0},{5,1},{6,2},{7,3},{8,12},{9,13},{10,... | collective-permute-start | bytes 393224 | tf_op jit(solution)/shard_map/ppermute | solution.py:380
  39.2 7.6 %collective-permute-start.3 = (f32[64,512]{1,0:T(8,128)S(1)}, f32[64,512]{1,0:T(8,128)S(1)}, u32[]{:S(2)}, u32[]{:S(2)}) collective-permute-start(f32[64,512]{1,0:T(8,128)S(1)} %shard_map.95.a_ref), channel_id=1, source_target_pairs={{0,2},{1,3},{2,0},{3,1},{4,6},{5,7},{6,4},{7,5},{8,10},{9,11},{10,... | collective-permute-start | bytes 393224 | tf_op jit(solution)/shard_map/ppermute | solution.py:387
  43.2 6.2 %collective-permute-start.2 = (f32[64,512]{1,0:T(8,128)S(1)}, f32[64,512]{1,0:T(8,128)S(1)}, u32[]{:S(2)}, u32[]{:S(2)}) collective-permute-start(f32[64,512]{1,0:T(8,128)S(1)} %shard_map.95.a_ref), channel_id=1, source_target_pairs={{0,3},{1,0},{2,1},{3,2},{4,7},{5,4},{6,5},{7,6},{8,11},{9,8},{10,9... | collective-permute-start | bytes 393224 | tf_op jit(solution)/shard_map/ppermute | solution.py:387
  43.9 6.2 %collective-permute-start.1 = (f32[64,512]{1,0:T(8,128)S(1)}, f32[64,512]{1,0:T(8,128)S(1)}, u32[]{:S(2)}, u32[]{:S(2)}) collective-permute-start(f32[64,512]{1,0:T(8,128)S(1)} %shard_map.95.a_ref), channel_id=1, source_target_pairs={{0,1},{1,2},{2,3},{3,0},{4,5},{5,6},{6,7},{7,4},{8,9},{9,10},{10,1... | collective-permute-start | bytes 393224 | tf_op jit(solution)/shard_map/ppermute | solution.py:387
  50.2 2.2 %collective-permute-start.4 = (bf16[64,512]{1,0:T(8,128)(2,1)S(1)}, bf16[64,512]{1,0:T(8,128)(2,1)S(1)}, u32[]{:S(2)}, u32[]{:S(2)}) collective-permute-start(bf16[64,512]{1,0:T(8,128)(2,1)S(1)} %get-tuple-element.21.latent_ref), channel_id=1, source_target_pairs={{0,8},{8,16},{16,24},{24,32},{32,40},{40,48},{48,56},{56,64},{64,7... | collective-permute-start | bytes 196616 | tf_op jit(solution)/shard_map/ppermute | solution.py:420
  61.8 27.9 %collective-permute-start.12 = (f32[8,8,4096]{2,1,0:T(8,128)S(1)}, f32[8,8,4096]{2,1,0:T(8,128)S(1)}, u32[]{:S(2)}, u32[]{:S(2)}) collective-permute-start(f32[8,8,4096]{2,1,0:T(8,128)S(1)} %get-tuple-element.27), channel_id=1, source_target_pairs={{0,8},{8,0},{16,24},{24,16},{32,40},{40,32},{48,56},{56,48},{64,72... | collective-permute-start | bytes 3145736 | tf_op jit(solution)/shard_map/ppermute | solution.py:299
  64.7 7.9 %collective-permute-start.7 = (f32[64,512]{1,0:T(8,128)S(1)}, f32[64,512]{1,0:T(8,128)S(1)}, u32[]{:S(2)}, u32[]{:S(2)}) collective-permute-start(f32[64,512]{1,0:T(8,128)S(1)} %get-tuple-element.23.a_ref), channel_id=1, source_target_pairs={{12,0},{13,1},{14,2},{15,3},{8,4},{9,5},{10,6},{11,7},{20,8},{21,9... | collective-permute-start | bytes 393224 | tf_op jit(solution)/shard_map/ppermute | solution.py:393
  66.0 6.6 %collective-permute-start.6 = (f32[64,512]{1,0:T(8,128)S(1)}, f32[64,512]{1,0:T(8,128)S(1)}, u32[]{:S(2)}, u32[]{:S(2)}) collective-permute-start(f32[64,512]{1,0:T(8,128)S(1)} %get-tuple-element.23.a_ref), channel_id=1, source_target_pairs={{8,0},{9,1},{10,2},{11,3},{12,4},{13,5},{14,6},{15,7},{16,8},{17,9... | collective-permute-start | bytes 393224 | tf_op jit(solution)/shard_map/ppermute | solution.py:393
  67.3 6.7 %collective-permute-start.5 = (f32[64,512]{1,0:T(8,128)S(1)}, f32[64,512]{1,0:T(8,128)S(1)}, u32[]{:S(2)}, u32[]{:S(2)}) collective-permute-start(f32[64,512]{1,0:T(8,128)S(1)} %get-tuple-element.23.a_ref), channel_id=1, source_target_pairs={{0,4},{1,5},{2,6},{3,7},{4,0},{5,1},{6,2},{7,3},{8,12},{9,13},{10,... | collective-permute-start | bytes 393224 | tf_op jit(solution)/shard_map/ppermute | solution.py:380
  74.0 6.6 %collective-permute-start.10 = (f32[64,512]{1,0:T(8,128)S(1)}, f32[64,512]{1,0:T(8,128)S(1)}, u32[]{:S(2)}, u32[]{:S(2)}) collective-permute-start(f32[64,512]{1,0:T(8,128)S(1)} %shard_map.97.a_ref), channel_id=1, source_target_pairs={{0,2},{1,3},{2,0},{3,1},{4,6},{5,7},{6,4},{7,5},{8,10},{9,11},{10,... | collective-permute-start | bytes 393224 | tf_op jit(solution)/shard_map/ppermute | solution.py:387
  75.9 6.1 %collective-permute-start.9 = (f32[64,512]{1,0:T(8,128)S(1)}, f32[64,512]{1,0:T(8,128)S(1)}, u32[]{:S(2)}, u32[]{:S(2)}) collective-permute-start(f32[64,512]{1,0:T(8,128)S(1)} %shard_map.97.a_ref), channel_id=1, source_target_pairs={{0,3},{1,0},{2,1},{3,2},{4,7},{5,4},{6,5},{7,6},{8,11},{9,8},{10,9... | collective-permute-start | bytes 393224 | tf_op jit(solution)/shard_map/ppermute | solution.py:387
  77.2 7.9 %collective-permute-start.8 = (f32[64,512]{1,0:T(8,128)S(1)}, f32[64,512]{1,0:T(8,128)S(1)}, u32[]{:S(2)}, u32[]{:S(2)}) collective-permute-start(f32[64,512]{1,0:T(8,128)S(1)} %shard_map.97.a_ref), channel_id=1, source_target_pairs={{0,1},{1,2},{2,3},{3,0},{4,5},{5,6},{6,7},{7,4},{8,9},{9,10},{10,1... | collective-permute-start | bytes 393224 | tf_op jit(solution)/shard_map/ppermute | solution.py:387
  87.1 2.9 %collective-permute-start.11 = (f32[8,8,4096]{2,1,0:T(8,128)S(1)}, f32[8,8,4096]{2,1,0:T(8,128)S(1)}, u32[]{:S(2)}, u32[]{:S(2)}) collective-permute-start(f32[8,8,4096]{2,1,0:T(8,128)S(1)} %encode_other_half.1), channel_id=1, source_target_pairs={{0,8},{8,0},{16,24},{24,16},{32,40},{40,32},{48,56},{56,48},{64,72... | collective-permute-start | bytes 3145736 | tf_op jit(solution)/shard_map/ppermute | solution.py:299
  90.2 15.8 %collective-permute-start.25 = (f32[2,2,2,8,1280]{4,3,2,1,0:T(8,128)S(1)}, f32[2,2,2,8,1280]{4,3,2,1,0:T(8,128)S(1)}, u32[]{:S(2)}, u32[]{:S(2)}) collective-permute-start(f32[2,2,2,8,1280]{4,3,2,1,0:T(8,128)S(1)} %fusion.15), channel_id=1, source_target_pairs={{0,96},{8,104},{16,112},{24,120},{32,64},{40,72},{48,80},{56,88},{... | collective-permute-start | bytes 983048 | tf_op jit(solution)/shard_map/ppermute | solution.py:295
  98.1 10.2 %collective-permute-start.13 = (f32[2,2,2,8,1408]{4,3,2,1,0:T(8,128)S(1)}, f32[2,2,2,8,1408]{4,3,2,1,0:T(8,128)S(1)}, u32[]{:S(2)}, u32[]{:S(2)}) collective-permute-start(f32[2,2,2,8,1408]{4,3,2,1,0:T(8,128)S(1)} %fusion.7), channel_id=1, source_target_pairs={{0,16},{8,24},{16,0},{24,8},{32,48},{40,56},{48,32},{56,40},{64,80... | collective-permute-start | bytes 1081352 | tf_op jit(solution)/shard_map/ppermute | solution.py:295
  99.0 10.9 %collective-permute-start.19 = (f32[2,2,2,8,1408]{4,3,2,1,0:T(8,128)S(1)}, f32[2,2,2,8,1408]{4,3,2,1,0:T(8,128)S(1)}, u32[]{:S(2)}, u32[]{:S(2)}) collective-permute-start(f32[2,2,2,8,1408]{4,3,2,1,0:T(8,128)S(1)} %fusion.6), channel_id=1, source_target_pairs={{0,32},{8,40},{16,48},{24,56},{32,0},{40,8},{48,16},{56,24},{64,96... | collective-permute-start | bytes 1081352 | tf_op jit(solution)/shard_map/ppermute | solution.py:295
  106.1 5.7 %collective-permute-start.26 = (f32[2,2,8,1280]{3,2,1,0:T(8,128)S(1)}, f32[2,2,8,1280]{3,2,1,0:T(8,128)S(1)}, u32[]{:S(2)}, u32[]{:S(2)}) collective-permute-start(f32[2,2,8,1280]{3,2,1,0:T(8,128)S(1)} %slice_bitcast_fusion.4), channel_id=1, source_target_pairs={{0,16},{8,24},{16,0},{24,8},{32,48},{40,56},{48,32},{56,40},{64,80... | collective-permute-start | bytes 491528 | tf_op jit(solution)/shard_map/ppermute | solution.py:295
  108.4 6.3 %collective-permute-start.14 = (f32[2,2,8,1408]{3,2,1,0:T(8,128)S(1)}, f32[2,2,8,1408]{3,2,1,0:T(8,128)S(1)}, u32[]{:S(2)}, u32[]{:S(2)}) collective-permute-start(f32[2,2,8,1408]{3,2,1,0:T(8,128)S(1)} %slice_bitcast_fusion.2), channel_id=1, source_target_pairs={{0,32},{8,40},{16,48},{24,56},{32,0},{40,8},{48,16},{56,24},{64,96... | collective-permute-start | bytes 540680 | tf_op jit(solution)/shard_map/ppermute | solution.py:295
  109.9 7.6 %collective-permute-start.20 = (f32[2,2,8,1408]{3,2,1,0:T(8,128)S(1)}, f32[2,2,8,1408]{3,2,1,0:T(8,128)S(1)}, u32[]{:S(2)}, u32[]{:S(2)}) collective-permute-start(f32[2,2,8,1408]{3,2,1,0:T(8,128)S(1)} %slice_bitcast_fusion), channel_id=1, source_target_pairs={{0,96},{8,104},{16,112},{24,120},{32,64},{40,72},{48,80},{56,88},{... | collective-permute-start | bytes 540680 | tf_op jit(solution)/shard_map/ppermute | solution.py:295
  111.9 5.8 %collective-permute-start.27 = (f32[2,8,1280]{2,1,0:T(8,128)S(1)}, f32[2,8,1280]{2,1,0:T(8,128)S(1)}, u32[]{:S(2)}, u32[]{:S(2)}) collective-permute-start(f32[2,8,1280]{2,1,0:T(8,128)S(1)} %slice_bitcast_fusion.10), channel_id=1, source_target_pairs={{0,32},{8,40},{16,48},{24,56},{32,0},{40,8},{48,16},{56,24},{64,96... | collective-permute-start | bytes 245768 | tf_op jit(solution)/shard_map/ppermute | solution.py:295
  114.7 5.8 %collective-permute-start.15 = (f32[2,8,1408]{2,1,0:T(8,128)S(1)}, f32[2,8,1408]{2,1,0:T(8,128)S(1)}, u32[]{:S(2)}, u32[]{:S(2)}) collective-permute-start(f32[2,8,1408]{2,1,0:T(8,128)S(1)} %slice_bitcast_fusion.8), channel_id=1, source_target_pairs={{0,96},{8,104},{16,112},{24,120},{32,64},{40,72},{48,80},{56,88},{... | collective-permute-start | bytes 270344 | tf_op jit(solution)/shard_map/ppermute | solution.py:295
  117.6 5.6 %collective-permute-start.21 = (f32[2,8,1408]{2,1,0:T(8,128)S(1)}, f32[2,8,1408]{2,1,0:T(8,128)S(1)}, u32[]{:S(2)}, u32[]{:S(2)}) collective-permute-start(f32[2,8,1408]{2,1,0:T(8,128)S(1)} %slice_bitcast_fusion.6), channel_id=1, source_target_pairs={{0,16},{8,24},{16,0},{24,8},{32,48},{40,56},{48,32},{56,40},{64,80... | collective-permute-start | bytes 270344 | tf_op jit(solution)/shard_map/ppermute | solution.py:295
  117.7 5.6 %collective-permute-start.28 = (f32[2,8,1280]{2,1,0:T(8,128)S(1)}, f32[2,8,1280]{2,1,0:T(8,128)S(1)}, u32[]{:S(2)}, u32[]{:S(2)}) collective-permute-start(f32[2,8,1280]{2,1,0:T(8,128)S(1)} %fusion.23), channel_id=1, source_target_pairs={{0,32},{8,40},{16,48},{24,56},{32,0},{40,8},{48,16},{56,24},{64,96... | collective-permute-start | bytes 245768 | tf_op jit(solution)/shard_map/ppermute | solution.py:295
  120.5 5.8 %collective-permute-start.16 = (f32[2,8,1408]{2,1,0:T(8,128)S(1)}, f32[2,8,1408]{2,1,0:T(8,128)S(1)}, u32[]{:S(2)}, u32[]{:S(2)}) collective-permute-start(f32[2,8,1408]{2,1,0:T(8,128)S(1)} %fusion.22), channel_id=1, source_target_pairs={{0,96},{8,104},{16,112},{24,120},{32,64},{40,72},{48,80},{56,88},{... | collective-permute-start | bytes 270344 | tf_op jit(solution)/shard_map/ppermute | solution.py:295
  123.2 4.6 %collective-permute-start.22 = (f32[2,8,1408]{2,1,0:T(8,128)S(1)}, f32[2,8,1408]{2,1,0:T(8,128)S(1)}, u32[]{:S(2)}, u32[]{:S(2)}) collective-permute-start(f32[2,8,1408]{2,1,0:T(8,128)S(1)} %fusion.21), channel_id=1, source_target_pairs={{0,16},{8,24},{16,0},{24,8},{32,48},{40,56},{48,32},{56,40},{64,80... | collective-permute-start | bytes 270344 | tf_op jit(solution)/shard_map/ppermute | solution.py:295
  123.3 11.4 %collective-permute-start.29 = (f32[2,2,8,1280]{3,2,1,0:T(8,128)S(1)}, f32[2,2,8,1280]{3,2,1,0:T(8,128)S(1)}, u32[]{:S(2)}, u32[]{:S(2)}) collective-permute-start(f32[2,2,8,1280]{3,2,1,0:T(8,128)S(1)} %get-tuple-element.41), channel_id=1, source_target_pairs={{0,16},{8,24},{16,0},{24,8},{32,48},{40,56},{48,32},{56,40},{64,80... | collective-permute-start | bytes 491528 | tf_op jit(solution)/shard_map/ppermute | solution.py:295
  126.4 6.1 %collective-permute-start.17 = (f32[2,2,8,1408]{3,2,1,0:T(8,128)S(1)}, f32[2,2,8,1408]{3,2,1,0:T(8,128)S(1)}, u32[]{:S(2)}, u32[]{:S(2)}) collective-permute-start(f32[2,2,8,1408]{3,2,1,0:T(8,128)S(1)} %get-tuple-element.39), channel_id=1, source_target_pairs={{0,32},{8,40},{16,48},{24,56},{32,0},{40,8},{48,16},{56,24},{64,96... | collective-permute-start | bytes 540680 | tf_op jit(solution)/shard_map/ppermute | solution.py:295
  127.8 6.8 %collective-permute-start.23 = (f32[2,2,8,1408]{3,2,1,0:T(8,128)S(1)}, f32[2,2,8,1408]{3,2,1,0:T(8,128)S(1)}, u32[]{:S(2)}, u32[]{:S(2)}) collective-permute-start(f32[2,2,8,1408]{3,2,1,0:T(8,128)S(1)} %get-tuple-element.37), channel_id=1, source_target_pairs={{0,96},{8,104},{16,112},{24,120},{32,64},{40,72},{48,80},{56,88},{... | collective-permute-start | bytes 540680 | tf_op jit(solution)/shard_map/ppermute | solution.py:295
  132.5 7.5 %collective-permute-start.31 = (f32[2,2,2,8,1408]{4,3,2,1,0:T(8,128)S(1)}, f32[2,2,2,8,1408]{4,3,2,1,0:T(8,128)S(1)}, u32[]{:S(2)}, u32[]{:S(2)}) collective-permute-start(f32[2,2,2,8,1408]{4,3,2,1,0:T(8,128)S(1)} %pad_maximum_fusion.2), channel_id=1, source_target_pairs={{0,16},{8,24},{16,0},{24,8},{32,48},{40,56},{48,32},{56,40},{64,80... | collective-permute-start | bytes 1081352 | tf_op jit(solution)/shard_map/ppermute | solution.py:295
  134.7 7.5 %collective-permute-start.33 = (f32[2,2,2,8,1408]{4,3,2,1,0:T(8,128)S(1)}, f32[2,2,2,8,1408]{4,3,2,1,0:T(8,128)S(1)}, u32[]{:S(2)}, u32[]{:S(2)}) collective-permute-start(f32[2,2,2,8,1408]{4,3,2,1,0:T(8,128)S(1)} %pad_maximum_fusion.3), channel_id=1, source_target_pairs={{0,32},{8,40},{16,48},{24,56},{32,0},{40,8},{48,16},{56,24},{64,96... | collective-permute-start | bytes 1081352 | tf_op jit(solution)/shard_map/ppermute | solution.py:295
  134.8 1.7 %collective-permute-start.30 = (f32[4,2,8,1280]{3,2,1,0:T(8,128)S(1)}, f32[4,2,8,1280]{3,2,1,0:T(8,128)S(1)}, u32[]{:S(2)}, u32[]{:S(2)}) collective-permute-start(f32[4,2,8,1280]{3,2,1,0:T(8,128)S(1)} %bitcast.114), channel_id=1, source_target_pairs={{0,8},{8,0},{16,24},{24,16},{32,40},{40,32},{48,56},{56,48},{64,72... | collective-permute-start | bytes 983048 | tf_op jit(solution)/shard_map/ppermute | solution.py:299
  134.9 11.3 %collective-permute-start.35 = (f32[2,2,2,8,1280]{4,3,2,1,0:T(8,128)S(1)}, f32[2,2,2,8,1280]{4,3,2,1,0:T(8,128)S(1)}, u32[]{:S(2)}, u32[]{:S(2)}) collective-permute-start(f32[2,2,2,8,1280]{4,3,2,1,0:T(8,128)S(1)} %pad_maximum_fusion.5), channel_id=1, source_target_pairs={{0,96},{8,104},{16,112},{24,120},{32,64},{40,72},{48,80},{56,88},{... | collective-permute-start | bytes 983048 | tf_op jit(solution)/shard_map/ppermute | solution.py:295
  136.4 9.8 %collective-permute-start.18 = (f32[4,2,8,1408]{3,2,1,0:T(8,128)S(1)}, f32[4,2,8,1408]{3,2,1,0:T(8,128)S(1)}, u32[]{:S(2)}, u32[]{:S(2)}) collective-permute-start(f32[4,2,8,1408]{3,2,1,0:T(8,128)S(1)} %bitcast.110), channel_id=1, source_target_pairs={{0,8},{8,0},{16,24},{24,16},{32,40},{40,32},{48,56},{56,48},{64,72... | collective-permute-start | bytes 1081352 | tf_op jit(solution)/shard_map/ppermute | solution.py:299
  136.5 9.7 %collective-permute-start.24 = (f32[4,2,8,1408]{3,2,1,0:T(8,128)S(1)}, f32[4,2,8,1408]{3,2,1,0:T(8,128)S(1)}, u32[]{:S(2)}, u32[]{:S(2)}) collective-permute-start(f32[4,2,8,1408]{3,2,1,0:T(8,128)S(1)} %bitcast.112), channel_id=1, source_target_pairs={{0,8},{8,0},{16,24},{24,16},{32,40},{40,32},{48,56},{56,48},{64,72... | collective-permute-start | bytes 1081352 | tf_op jit(solution)/shard_map/ppermute | solution.py:299
  140.0 8.5 %collective-permute-start.32 = (f32[4,2,8,1408]{3,2,1,0:T(8,128)S(1)}, f32[4,2,8,1408]{3,2,1,0:T(8,128)S(1)}, u32[]{:S(2)}, u32[]{:S(2)}) collective-permute-start(f32[4,2,8,1408]{3,2,1,0:T(8,128)S(1)} %bitcast.118), channel_id=1, source_target_pairs={{0,8},{8,0},{16,24},{24,16},{32,40},{40,32},{48,56},{56,48},{64,72... | collective-permute-start | bytes 1081352 | tf_op jit(solution)/shard_map/ppermute | solution.py:299
  142.2 6.4 %collective-permute-start.34 = (f32[4,2,8,1408]{3,2,1,0:T(8,128)S(1)}, f32[4,2,8,1408]{3,2,1,0:T(8,128)S(1)}, u32[]{:S(2)}, u32[]{:S(2)}) collective-permute-start(f32[4,2,8,1408]{3,2,1,0:T(8,128)S(1)} %bitcast.120), channel_id=1, source_target_pairs={{0,8},{8,0},{16,24},{24,16},{32,40},{40,32},{48,56},{56,48},{64,72... | collective-permute-start | bytes 1081352 | tf_op jit(solution)/shard_map/ppermute | solution.py:299
  146.2 2.3 %collective-permute-start.36 = (f32[4,2,8,1280]{3,2,1,0:T(8,128)S(1)}, f32[4,2,8,1280]{3,2,1,0:T(8,128)S(1)}, u32[]{:S(2)}, u32[]{:S(2)}) collective-permute-start(f32[4,2,8,1280]{3,2,1,0:T(8,128)S(1)} %bitcast.122), channel_id=1, source_target_pairs={{0,8},{8,0},{16,24},{24,16},{32,40},{40,32},{48,56},{56,48},{64,72... | collective-permute-start | bytes 983048 | tf_op jit(solution)/shard_map/ppermute | solution.py:299
